TPU v7x, 256 devices: a whole 4x4x8 slice. The times are simulated.
256 devices in a mesh: grp: 8 (over z), exp: 16 (over x, y), rep: 2 (over core).
Axes of the slice: x: 4, y: 4, z: 8, core: 2. Of those that a mesh axis runs over, the one named last changes fastest.
Arguments:
- tokens: bfloat16 [8192, 2048], P(('grp', 'exp', 'rep')), may hold values from -6 to 6
- cotangent: bfloat16 [8192, 2048], P(('grp', 'exp', 'rep')), may hold values from -6 to 6
- expert_ids: int32 [8192, 8], P(('grp', 'exp', 'rep')), may hold values from 0 to 127, all different within a row; in each aligned block of 32 rows (0 to 31, 32 to 63, ...) at most 3 rows name the same one
- gate_probs: float32 [8192, 8], P(('grp', 'exp', 'rep')), may hold values from 0.05 to 0.6
- gate_weight: bfloat16 [128, 2048, 768], P(('grp', 'exp'), 'rep'), may hold values from -0.125 to 0.125
- up_weight: bfloat16 [128, 2048, 768], P(('grp', 'exp'), 'rep'), may hold values from -0.125 to 0.125
- down_weight: bfloat16 [128, 768, 2048], P(('grp', 'exp'), 'rep'), may hold values from -0.21875 to 0.21875
Outputs:
- layer_out: bfloat16 [8192, 2048], P(('grp', 'exp', 'rep'))
- token_grad: bfloat16 [8192, 2048], P(('grp', 'exp', 'rep'))
- gate_grad: bfloat16 [128, 2048, 768], P(('grp', 'exp'), 'rep')
- up_grad: bfloat16 [128, 2048, 768], P(('grp', 'exp'), 'rep')
- down_grad: bfloat16 [128, 768, 2048], P(('grp', 'exp'), 'rep')
Inputs may be any that keep to these rules, and one draw needn't show every extreme that they name: `expert_ids`: each token names 8 different experts. Among the 32 tokens of one device, no expert is named more than 3 times, and in some device one expert is named exactly 3 times.
All inputs are finite; a program needn't handle non-finite values.
Results may differ from a plain program's by a relative error of at most 0.0065.
Values may be sent and summed in bfloat16 or wider, within the bound.
A program may use at most 128 MiB of HBM per device.

v0:
```python
import jax
import jax.numpy as jnp
from jax import lax
from jax.sharding import PartitionSpec as P

TOP = 8


def in_one_piece(arrays, axis, dim, along):
    both = jnp.concatenate(arrays, axis=along)
    filled, at, done = (lax.all_gather(both, axis, axis=dim, tiled=True), 0, [])
    for a in arrays:
        done.append(lax.slice_in_dim(filled, at, at + a.shape[along], axis=along))
        at += a.shape[along]
    return tuple(done)


def side_by_side(arrays, axis, split_dim, concat_dim, along):
    ends, at = ([], 0)
    for a in arrays[:-1]:
        at += a.shape[along]
        ends.append(at)
    both = jnp.concatenate(arrays, axis=along)
    return tuple(
        jnp.split(
            lax.all_to_all(both, axis, split_axis=split_dim, concat_axis=concat_dim, tiled=True),
            ends,
            axis=along,
        )
    )


def partner_2(value, axis, bit):
    mask = 2**bit
    pairs = [(source, source ^ mask) for source in range(lax.axis_size(axis))]
    return lax.ppermute(value, axis, pairs)


def contract_rows(left, right):
    return lax.dot_general(
        left, right, (((0,), (0,)), ((), ())), preferred_element_type=jnp.float32
    )


def contract_cols(left, right):
    return lax.dot_general(
        left, right, (((1,), (1,)), ((), ())), preferred_element_type=jnp.float32
    )


def rounded_sum(first, second):
    left_part = lax.optimization_barrier(first.astype(jnp.bfloat16))
    right_part = lax.optimization_barrier(second.astype(jnp.bfloat16))
    return left_part.astype(jnp.float32) + right_part.astype(jnp.float32)


def local(tokens, cotangent, expert_ids, gate_probs, gate_weight, up_weight, down_weight):
    group_count = lax.axis_size("grp")
    inner_count = lax.axis_size("exp")
    expert_count = group_count * inner_count
    token_count = tokens.shape[0]
    model_width = tokens.shape[1]
    capacity = 3 * token_count * TOP // (2 * expert_count)
    slot_count = expert_count * capacity
    row_count = token_count * TOP
    flat_ids = expert_ids.reshape(row_count)
    flat_probs = gate_probs.reshape(row_count)
    one_hot = (flat_ids[:, None] == jnp.arange(expert_count, dtype=jnp.int32)[None, :]).astype(
        jnp.float32
    )
    earlier = (jnp.arange(row_count)[:, None] > jnp.arange(row_count)[None, :]).astype(jnp.float32)
    counted = jnp.dot(earlier, one_hot, precision=lax.Precision.HIGHEST)
    slot_rank = jnp.sum(counted * one_hot, axis=1).astype(jnp.int32)
    target = flat_ids * capacity + slot_rank
    picked = jnp.arange(slot_count, dtype=jnp.int32)[:, None] == target[None, :]
    slot_probs = jnp.dot(picked.astype(jnp.float32), flat_probs, precision=lax.Precision.HIGHEST)
    pick_tokens = picked.reshape(slot_count, token_count, TOP).any(axis=2).astype(jnp.bfloat16)
    send_tokens = jnp.dot(pick_tokens, tokens, preferred_element_type=jnp.float32).astype(
        jnp.bfloat16
    )
    send_scaled = (
        jnp.dot(pick_tokens, cotangent, preferred_element_type=jnp.float32) * slot_probs[:, None]
    ).astype(jnp.bfloat16)
    whole = (
        *in_one_piece((gate_weight, up_weight), "rep", 1, 0),
        lax.all_gather(down_weight, "rep", axis=1, tiled=True),
    )
    gate_mat = whole[0][0]
    up_mat = whole[1][0]
    down_mat = whole[2][0]
    arrived = (
        lax.all_to_all(
            send_tokens.reshape(expert_count, capacity, model_width),
            ("grp", "exp"),
            split_axis=0,
            concat_axis=0,
            tiled=True,
        ),
        lax.all_to_all(
            send_scaled.reshape(expert_count, capacity, model_width),
            ("grp", "exp"),
            split_axis=0,
            concat_axis=0,
            tiled=True,
        ),
    )
    rows_in = arrived[0].reshape(slot_count, model_width)
    rows_scaled = arrived[1].reshape(slot_count, model_width)
    gate_pre = jnp.dot(rows_in, gate_mat, preferred_element_type=jnp.float32)
    up_pre = jnp.dot(rows_in, up_mat, preferred_element_type=jnp.float32)
    sigma = jax.nn.sigmoid(gate_pre)
    act = gate_pre * sigma
    hidden = (act * up_pre).astype(jnp.bfloat16)
    out_rows = jnp.dot(hidden, down_mat, preferred_element_type=jnp.float32).astype(jnp.bfloat16)
    dhidden = contract_cols(rows_scaled, down_mat)
    dgate = (dhidden * up_pre * sigma * (1.0 + gate_pre * (1.0 - sigma))).astype(jnp.bfloat16)
    dup = (dhidden * act).astype(jnp.bfloat16)
    grad_rows = (contract_cols(dgate, gate_mat) + contract_cols(dup, up_mat)).astype(jnp.bfloat16)
    returned = side_by_side(
        (
            out_rows.reshape(expert_count, capacity, model_width),
            grad_rows.reshape(expert_count, capacity, model_width),
        ),
        ("grp", "exp"),
        0,
        0,
        1,
    )
    replica = lax.axis_index("rep")
    other = 1 - replica
    half_width = gate_weight.shape[1]
    half_hidden = down_weight.shape[1]
    own_in = lax.dynamic_slice_in_dim(rows_in, replica * half_width, half_width, 1)
    own_hidden = lax.dynamic_slice_in_dim(hidden, replica * half_hidden, half_hidden, 1)
    send_in = lax.dynamic_slice_in_dim(rows_in, other * half_width, half_width, 1)
    send_hidden = lax.dynamic_slice_in_dim(hidden, other * half_hidden, half_hidden, 1)
    partner = partner_2((send_in, rows_scaled, send_hidden, dgate, dup), "rep", 0)
    gate_out = rounded_sum(contract_rows(own_in, dgate), contract_rows(partner[0], partner[3]))[
        None
    ]
    up_out = rounded_sum(contract_rows(own_in, dup), contract_rows(partner[0], partner[4]))[None]
    down_out = rounded_sum(
        contract_rows(own_hidden, rows_scaled), contract_rows(partner[2], partner[1])
    )[None]
    back_out = returned[0].reshape(slot_count, model_width)
    back_grad = returned[1].reshape(slot_count, model_width)
    route_out = jnp.dot(picked.T.astype(jnp.bfloat16), back_out, preferred_element_type=jnp.float32)
    layer_out = jnp.sum(
        route_out.reshape(token_count, TOP, model_width) * gate_probs[:, :, None], axis=1
    )
    token_grad = jnp.dot(pick_tokens.T, back_grad, preferred_element_type=jnp.float32)
    return (
        layer_out.astype(jnp.bfloat16),
        token_grad.astype(jnp.bfloat16),
        gate_out.astype(jnp.bfloat16),
        up_out.astype(jnp.bfloat16),
        down_out.astype(jnp.bfloat16),
    )


def solution(mesh):
    in_specs = (
        P(("grp", "exp", "rep"), None),
        P(("grp", "exp", "rep"), None),
        P(("grp", "exp", "rep"), None),
        P(("grp", "exp", "rep"), None),
        P(("grp", "exp"), "rep", None),
        P(("grp", "exp"), "rep", None),
        P(("grp", "exp"), "rep", None),
    )
    out_specs = (
        P(("grp", "exp", "rep"), None),
        P(("grp", "exp", "rep"), None),
        P(("grp", "exp"), "rep", None),
        P(("grp", "exp"), "rep", None),
        P(("grp", "exp"), "rep", None),
    )
    return jax.shard_map(local, mesh=mesh, in_specs=in_specs, out_specs=out_specs, check_vma=False)
```

profile of v0, /device:TPU:2, one launch (start us, length us, event | category | flops | bytes accessed | tf_op | source)
XLA Modules:
  0.0 305.9 jit_solution(10016132860593222310)
XLA Ops:
  9.3 2.4 reshape.93
  11.7 15.4 %all-to-all-start = ((bf16[128,3,2048]{2,1,0:T(4,128)(2,1)}), bf16[128,3,2048]{2,1,0:T(4,128)(2,1)S(1)}, u32[]{:S(2)}, u32[]{:S(2)}) async-start(bf16[128,3,2048]{2,1,0:T(4,128)(2,1)} %reshape.93), calls=%async_computation | async-start | bytes 4194304 | tf_op jit(solution)/shard_map/all_to_all | solution.py:92
  27.2 4.3 %pad_maximum_fusion.1 = bf16[2,1024,768]{2,1,0:T(8,128)(2,1)} fusion(bf16[1,1024,768]{2,1,0:T(8,128)(2,1)} %param.12, bf16[1,1024,768]{2,1,0:T(8,128)(2,1)} %param.11), kind=kLoop, calls=%fused_computation.3 | loop fusion | flops 1572864 | bytes 6291456 | tf_op jit(solution)/shard_map/concatenate | solution.py:10
  34.4 5.2 %reshape.97 = bf16[128,3,2048]{2,1,0:T(4,128)(2,1)} reshape(bf16[384,2048]{1,0:T(8,128)(2,1)} %multiply_convert_fusion) | data formatting | bytes 3145728 | tf_op jit(solution)/shard_map/reshape | solution.py:100
  39.6 40.1 %all-to-all-done = bf16[128,3,2048]{2,1,0:T(4,128)(2,1)S(1)} async-done(((bf16[128,3,2048]{2,1,0:T(4,128)(2,1)}), bf16[128,3,2048]{2,1,0:T(4,128)(2,1)S(1)}, u32[]{:S(2)}, u32[]{:S(2)}) %all-to-all-start) | async-done | bytes 1572896 | tf_op jit(solution)/shard_map/all_to_all | solution.py:92
  79.7 7.8 %all-to-all-start.1 = ((bf16[128,3,2048]{2,1,0:T(4,128)(2,1)}), bf16[128,3,2048]{2,1,0:T(4,128)(2,1)}, u32[]{:S(2)}, u32[]{:S(2)}) async-start(bf16[128,3,2048]{2,1,0:T(4,128)(2,1)} %reshape.97), calls=%async_computation.1 | async-start | bytes 4194304 | tf_op jit(solution)/shard_map/all_to_all | solution.py:99
  87.5 2.5 reshape.94
  90.0 49.1 %all-to-all-done.1 = bf16[128,3,2048]{2,1,0:T(4,128)(2,1)} async-done(((bf16[128,3,2048]{2,1,0:T(4,128)(2,1)}), bf16[128,3,2048]{2,1,0:T(4,128)(2,1)}, u32[]{:S(2)}, u32[]{:S(2)}) %all-to-all-start.1) | async-done | bytes 1572896 | tf_op jit(solution)/shard_map/all_to_all | solution.py:99
  139.1 3.9 %reshape.98 = bf16[384,2048]{1,0:T(8,128)(2,1)S(1)} reshape(bf16[128,3,2048]{2,1,0:T(4,128)(2,1)} %all-to-all-done.1) | data formatting | bytes 3145728 | tf_op jit(solution)/shard_map/reshape | solution.py:108
  143.0 4.9 %fusion = f32[384,768]{1,0:T(8,128)} fusion(bf16[384,2048]{1,0:T(8,128)(2,1)S(1)} %reshape.98, bf16[1,768,2048]{2,1,0:T(8,128)(2,1)} %all-gather.5.cloned.1.call-done), kind=kOutput, calls=%fused_computation.4 | convolution fusion | flops 1207959552 | bytes 5898240 | tf_op jit(solution)/shard_map/dot_general | solution.py:46
  148.0 3.4 %fusion.8 = f32[384,768]{1,0:T(8,128)S(1)} fusion(bf16[384,2048]{1,0:T(8,128)(2,1)S(1)} %copy-done.2, bf16[2,2048,768]{2,1,0:T(8,128)(2,1)} %all-gather.3.cloned.1.call-done), kind=kOutput, calls=%fused_computation.18 | convolution fusion | flops 1207959552 | bytes 5898240 | tf_op jit(solution)/shard_map/dot_general | solution.py:109
  155.2 2.6 add_convert_fusion.3
  157.8 4.0 %reshape.99 = bf16[128,3,2048]{2,1,0:T(4,128)(2,1)S(1)} reshape(bf16[384,2048]{1,0:T(8,128)(2,1)} %add_convert_fusion.3) | data formatting | bytes 3145728 | tf_op jit(solution)/shard_map/reshape | solution.py:122
  161.8 4.4 %fusion.4 = bf16[384,2048]{1,0:T(8,128)(2,1)} fusion(bf16[384,768]{1,0:T(8,128)(2,1)S(1)} %get-tuple-element.7, bf16[1,768,2048]{2,1,0:T(8,128)(2,1)} %all-gather.5.cloned.1.call-done), kind=kOutput, calls=%fused_computation.13 | convolution fusion | flops 1208745984 | bytes 5308416 | tf_op jit(solution)/shard_map/dot_general | solution.py:114
  166.2 5.2 %reshape.95 = bf16[128,3,2048]{2,1,0:T(4,128)(2,1)} reshape(bf16[384,2048]{1,0:T(8,128)(2,1)} %fusion.4) | data formatting | bytes 3145728 | tf_op jit(solution)/shard_map/reshape | solution.py:121
  171.3 4.8 %pad_maximum_fusion = bf16[128,6,2048]{2,1,0:T(8,128)(2,1)} fusion(bf16[128,3,2048]{2,1,0:T(4,128)(2,1)S(1)} %reshape.99, bf16[128,3,2048]{2,1,0:T(4,128)(2,1)} %reshape.95), kind=kLoop, calls=%fused_computation | loop fusion | flops 6291456 | bytes 6291456 | tf_op jit(solution)/shard_map/concatenate | solution.py:23
  176.1 7.9 %all-to-all-start.2 = ((bf16[128,6,2048]{2,1,0:T(8,128)(2,1)}), bf16[128,6,2048]{2,1,0:T(8,128)(2,1)}, u32[]{:S(2)}, u32[]{:S(2)}) async-start(bf16[128,6,2048]{2,1,0:T(8,128)(2,1)} %pad_maximum_fusion), calls=%async_computation.2 | async-start | bytes 8388608 | tf_op jit(solution)/shard_map/all_to_all | solution.py:26
  191.0 2.4 convolution_convert_fusion
  200.4 78.8 %all-to-all-done.2 = bf16[128,6,2048]{2,1,0:T(8,128)(2,1)} async-done(((bf16[128,6,2048]{2,1,0:T(8,128)(2,1)}), bf16[128,6,2048]{2,1,0:T(8,128)(2,1)}, u32[]{:S(2)}, u32[]{:S(2)}) %all-to-all-start.2) | async-done | bytes 3145760 | tf_op jit(solution)/shard_map/all_to_all | solution.py:26
  279.2 6.8 %fusion.28 = (bf16[128,3,2048]{2,1,0:T(4,128)(2,1)S(1)}, bf16[128,3,2048]{2,1,0:T(4,128)(2,1)}) fusion(bf16[128,6,2048]{2,1,0:T(8,128)(2,1)} %all-to-all-done.2), kind=kLoop, calls=%fused_computation.58 | loop fusion | bytes 6291456 | tf_op jit(solution)/shard_map/split | solution.py:25
  286.0 5.0 %reshape.104 = bf16[384,2048,1]{1,0,2:T(8,128)(2,1)} reshape(bf16[128,3,2048]{2,1,0:T(4,128)(2,1)} %get-tuple-element.6) | data formatting | bytes 3145728 | tf_op jit(solution)/shard_map/reshape | solution.py:145
  291.0 3.1 %fusion.13 = bf16[32,2048]{1,0:T(8,128)(2,1)} fusion(bf16[384,2048,1]{1,0,2:T(8,128)(2,1)} %reshape.104, f32[32,8]{1,0:T(8,128)S(1)} %copy.20, s32[256]{0:T(256)S(1)} %multiply_add_fusion.1), kind=kOutput, calls=%fused_computation.29 | convolution fusion | flops 403734528 | bytes 1705984 | tf_op jit(solution)/shard_map/dot_general | solution.py:147
  294.1 2.5 reshape.101
  296.6 2.4 convolution_convert_fusion.3
  (75 shorter events, 22.6 us)
Async XLA Ops:
  7.2 1.5 copy-start
  7.2 135.8 %all-gather.5.cloned.1.call-start = ((), (), s32[]{:S(2)}) async-start(), calls=%async_computation.4 | async-start | bytes 4718592 | tf_op jit(solution)/shard_map/all_gather | solution.py:86
  11.7 68.0 %all-to-all-start = ((bf16[128,3,2048]{2,1,0:T(4,128)(2,1)}), bf16[128,3,2048]{2,1,0:T(4,128)(2,1)S(1)}, u32[]{:S(2)}, u32[]{:S(2)}) async-start(bf16[128,3,2048]{2,1,0:T(4,128)(2,1)} %reshape.93), calls=%async_computation | async-start | bytes 4194304 | tf_op jit(solution)/shard_map/all_to_all | solution.py:92
  27.1 120.9 %all-gather.3.cloned.1.call-start = ((), (), s32[]{:S(2)}) async-start(), calls=%async_computation.3 | async-start | bytes 9437184 | tf_op jit(solution)/shard_map/all_gather | solution.py:11
  31.5 1.2 copy-start.8
  79.7 59.4 %all-to-all-start.1 = ((bf16[128,3,2048]{2,1,0:T(4,128)(2,1)}), bf16[128,3,2048]{2,1,0:T(4,128)(2,1)}, u32[]{:S(2)}, u32[]{:S(2)}) async-start(bf16[128,3,2048]{2,1,0:T(4,128)(2,1)} %reshape.97), calls=%async_computation.1 | async-start | bytes 4194304 | tf_op jit(solution)/shard_map/all_to_all | solution.py:99
  143.0 5.0 %copy-start.4 = (bf16[384,2048]{1,0:T(8,128)(2,1)}, bf16[384,2048]{1,0:T(8,128)(2,1)S(1)}, u32[]{:S(2)}) copy-start(bf16[384,2048]{1,0:T(8,128)(2,1)S(1)} %reshape.98) | copy-start | bytes 4718596
  143.0 5.0 %copy-start.2 = (bf16[384,2048]{1,0:T(8,128)(2,1)S(1)}, bf16[384,2048]{1,0:T(8,128)(2,1)}, u32[]{:S(2)}) copy-start(bf16[384,2048]{1,0:T(8,128)(2,1)} %reshape.94) | copy-start | bytes 4718596
  148.0 3.7 %copy-start.11 = (bf16[2,2048,768]{2,1,0:T(8,128)(2,1)S(1)}, bf16[2,2048,768]{2,1,0:T(8,128)(2,1)}, u32[]{:S(2)}) copy-start(bf16[2,2048,768]{2,1,0:T(8,128)(2,1)} %all-gather.3.cloned.1.call-done) | copy-start | bytes 18874372
  148.0 4.0 %copy-start.16 = (f32[384,768]{1,0:T(8,128)S(1)}, f32[384,768]{1,0:T(8,128)}, u32[]{:S(2)}) copy-start(f32[384,768]{1,0:T(8,128)} %fusion) | copy-start | bytes 3538948
  153.7 1.5 copy-start.14
  153.7 1.5 copy-start.12
  153.7 8.0 %copy-start.6 = (bf16[384,768]{1,0:T(8,128)(2,1)}, bf16[384,768]{1,0:T(8,128)(2,1)S(1)}, u32[]{:S(2)}) copy-start(bf16[384,768]{1,0:T(8,128)(2,1)S(1)} %get-tuple-element.7) | copy-start | bytes 1769476
  176.1 7.9 %copy-start.5 = (bf16[384,2048]{1,0:T(8,128)(2,1)S(1)}, bf16[384,2048]{1,0:T(8,128)(2,1)}, u32[]{:S(2)}) copy-start(bf16[384,2048]{1,0:T(8,128)(2,1)} %copy-done.4) | copy-start | bytes 4718596
  176.1 8.3 %copy-start.3 = (bf16[384,2048]{1,0:T(8,128)(2,1)S(1)}, bf16[384,2048]{1,0:T(8,128)(2,1)}, u32[]{:S(2)}) copy-start(bf16[384,2048]{1,0:T(8,128)(2,1)} %reshape.94) | copy-start | bytes 4718596
  176.1 103.1 %all-to-all-start.2 = ((bf16[128,6,2048]{2,1,0:T(8,128)(2,1)}), bf16[128,6,2048]{2,1,0:T(8,128)(2,1)}, u32[]{:S(2)}, u32[]{:S(2)}) async-start(bf16[128,6,2048]{2,1,0:T(8,128)(2,1)} %pad_maximum_fusion), calls=%async_computation.2 | async-start | bytes 8388608 | tf_op jit(solution)/shard_map/all_to_all | solution.py:26
  184.0 5.7 %collective-permute-start.4 = (bf16[384,2048]{1,0:T(8,128)(2,1)S(1)}, bf16[384,2048]{1,0:T(8,128)(2,1)}, u32[]{:S(2)}, u32[]{:S(2)}) collective-permute-start(bf16[384,2048]{1,0:T(8,128)(2,1)S(1)} %copy-done.5), channel_id=1, source_target_pairs={{0,1},{1,0},{2,3},{3,2},{4,5},{5,4},{6,7},{7,6},{8,9},{9,8},{10,11... | collective-permute-start | bytes 4718600 | tf_op jit(solution)/shard_map/ppermute | solution.py:36
  184.4 1.1 copy-start.15
  184.4 1.5 copy-start.13
  184.5 10.7 %collective-permute-start = (bf16[384,1024]{1,0:T(8,128)(2,1)S(1)}, bf16[384,1024]{1,0:T(8,128)(2,1)S(1)}, u32[]{:S(2)}, u32[]{:S(2)}) collective-permute-start(bf16[384,1024]{1,0:T(8,128)(2,1)S(1)} %constant_dynamic-slice_fusion.1), channel_id=1, source_target_pairs={{0,1},{1,0},{2,3},{3,2},{4,5},{5,4},{6,7},{7,6},{8,9},{9,8},{10,11... | collective-permute-start | bytes 2359304 | tf_op jit(solution)/shard_map/ppermute | solution.py:36
  185.4 9.7 %collective-permute-start.1 = (bf16[384,768]{1,0:T(8,128)(2,1)S(1)}, bf16[384,768]{1,0:T(8,128)(2,1)S(1)}, u32[]{:S(2)}, u32[]{:S(2)}) collective-permute-start(bf16[384,768]{1,0:T(8,128)(2,1)S(1)} %copy-done.15), channel_id=1, source_target_pairs={{0,1},{1,0},{2,3},{3,2},{4,5},{5,4},{6,7},{7,6},{8,9},{9,8},{10,11... | collective-permute-start | bytes 1769480 | tf_op jit(solution)/shard_map/ppermute | solution.py:36
  185.9 10.3 %collective-permute-start.2 = (bf16[384,768]{1,0:T(8,128)(2,1)S(1)}, bf16[384,768]{1,0:T(8,128)(2,1)S(1)}, u32[]{:S(2)}, u32[]{:S(2)}) collective-permute-start(bf16[384,768]{1,0:T(8,128)(2,1)S(1)} %copy-done.13), channel_id=1, source_target_pairs={{0,1},{1,0},{2,3},{3,2},{4,5},{5,4},{6,7},{7,6},{8,9},{9,8},{10,11... | collective-permute-start | bytes 1769480 | tf_op jit(solution)/shard_map/ppermute | solution.py:36
  188.3 2.7 collective-permute-start.3
  294.1 4.9 %copy-start.1 = (bf16[32,2048]{1,0:T(8,128)(2,1)S(1)}, bf16[32,2048]{1,0:T(8,128)(2,1)}, u32[]{:S(2)}) copy-start(bf16[32,2048]{1,0:T(8,128)(2,1)} %param.7) | copy-start | bytes 393220
  (3 other events, 2.5 us)
Sparse Core Ops, SparseCore 0:
  9.8 20.3 all-gather.4
  32.0 23.3 all-gather.2
where the time goes:
time: 307 us; the launch traced here: 306 us
  waiting for transfers between devices  170 us (55%)
  local copies, waits for them, and re-layouts  39.7 us (13%)
  matrix products  34.4 us (11%)
  starting transfers between devices  33.1 us (11%)
  between operations  14.4 us (5%)
  other arithmetic  14.2 us (5%)
    all_to_all x1, waiting for transfers between devices, side_by_side(): lax.all_to_all(both, axis, split_axis=split_dim, concat_axis=concat_dim,...  78.8 us
    all_to_all x1, waiting for transfers between devices, local(): lax.all_to_all(send_scaled.reshape(expert_count, capacity, model_width),...  49.1 us
    all_to_all x1, waiting for transfers between devices, local(): lax.all_to_all(send_tokens.reshape(expert_count, capacity, model_width),...  40.1 us
    all_to_all x1, starting transfers between devices, local(): lax.all_to_all(send_tokens.reshape(expert_count, capacity, model_width),...  15.4 us
    dot_general x3, matrix products, contract_cols(): lax.dot_general(left, right, (((1,), (1,)), ((), ())), preferred_element_...  8.9 us
    all_to_all x1, starting transfers between devices, side_by_side(): lax.all_to_all(both, axis, split_axis=split_dim, concat_axis=concat_dim,...  7.9 us
    all_to_all x1, starting transfers between devices, local(): lax.all_to_all(send_scaled.reshape(expert_count, capacity, model_width),...  7.79 us
    dot_general x6, matrix products, contract_rows(): lax.dot_general(left, right, (((0,), (0,)), ((), ())), preferred_element_...  7.54 us
  transfers between devices with their start and end apart: 10, of which 4 were waited for; matrix products, arithmetic and copies ran while one was open for 13% of the time, Pallas kernels for 0%

commit v1 on v0

v1 whole, which is shorter than its diff:
```python
import functools

import jax
import jax.numpy as jnp
from jax import lax
from jax.experimental import pallas as pl
from jax.experimental.pallas import tpu as pltpu
from jax.sharding import PartitionSpec as P

MESH = pl.DeviceIdType.MESH
F32 = jnp.float32
BF16 = jnp.bfloat16
RANKS = 3
HALF = 4
PIECES = 2 * HALF


def dot(a, b, dims):
    return lax.dot_general(a, b, (dims, ((), ())), preferred_element_type=F32)


NN = ((1,), (0,))
NT = ((1,), (1,))
TN = ((0,), (0,))


def kernel(
    zn, en,
    tok, cot, meta, wg, wu, wd,
    out_y, out_dx, out_g, out_u, out_d,
    ag, meta_v, wg_v, wu_v, wd_v, rank_v, prob_v, pick_f, prob_f, pick_b, pick_t, hi_t, lo_t,
    send, recv, gate, up, dh, hid, dgu, back, ret, part, rs_s, rs_r, own_gu, own_d, snd_gu, snd_d,
    rcv_gu, rcv_d, y_v, dx_v,
    l_sem, lm_sem, lw_sem, m_ssem, m_rsem, w_ssem, w_rsem, ag_ssem, ag_rsem, d_ssem, d_rsem, own_sem,
    b_ssem, b_rsem, bown_sem, rs_ssem, rs_rsem, g_ssem, g_rsem, o_sem,
):
    z = lax.axis_index("grp")
    c = lax.axis_index("exp")
    r = lax.axis_index("rep")
    o = 1 - r
    tn = ag.shape[2]
    w = ag.shape[3]
    rows = RANKS * zn
    slots = en * rows
    ff = gate.shape[1]
    fh = ff // 2
    lanes = 128
    per = lanes // tn
    long = zn // 2

    def hops(p, way):
        return long if (p % 2) == way else zn - 1 - long

    def step(way):
        return 1 if way == 0 else -1

    def there(way):
        return {"grp": lax.rem(z + step(way) + zn, zn)}

    def local(p):
        src = tok if p < HALF else cot
        return pltpu.make_async_copy(
            src.at[:, pl.ds((p % HALF) * w, w)], ag.at[p, z], l_sem.at[p])

    meta_in = pltpu.make_async_copy(meta, meta_v.at[z], lm_sem)
    meta_in.start()
    for p in range(PIECES):
        local(p).start()
    wq = HALF // 2
    half_gate = pl.ds(r * wq, wq)
    half_down = pl.ds(pl.multiple_of(r * fh, fh), fh)
    w_local = [
        pltpu.make_async_copy(wg, wg_v.at[half_gate], lw_sem.at[0]),
        pltpu.make_async_copy(wu, wu_v.at[half_gate], lw_sem.at[1]),
    ]
    for q in range(HALF):
        w_local.append(pltpu.make_async_copy(
            wd.at[:, pl.ds(q * w, w)], wd_v.at[q, half_down], lw_sem.at[2 + q]))
    for copy in w_local:
        copy.start()

    barrier = pltpu.get_barrier_semaphore()
    pl.semaphore_signal(barrier, inc=1, device_id={"rep": o}, device_id_type=MESH)

    def greet_grp(d, carry):
        pl.semaphore_signal(barrier, inc=1, device_id={"grp": lax.rem(z + d, zn)}, device_id_type=MESH)
        return carry

    def greet_exp(d, carry):
        pl.semaphore_signal(barrier, inc=1, device_id={"exp": lax.rem(c + d, en)}, device_id_type=MESH)
        return carry

    lax.fori_loop(1, zn, greet_grp, 0)
    lax.fori_loop(1, en, greet_exp, 0)
    pl.semaphore_wait(barrier, 1 + (zn - 1) + (en - 1))

    meta_in.wait()

    def send_meta(d, carry):
        pltpu.make_async_remote_copy(
            src_ref=meta_v.at[z], dst_ref=meta_v.at[z], send_sem=m_ssem, recv_sem=m_rsem,
            device_id={"grp": lax.rem(z + d, zn)}, device_id_type=MESH).start()
        return carry

    lax.fori_loop(1, zn, send_meta, 0)

    def ring(p, way, s):
        block = lax.rem(z - step(way) * s + zn, zn)
        return pltpu.make_async_remote_copy(
            src_ref=ag.at[p, block], dst_ref=ag.at[p, block],
            send_sem=ag_ssem.at[way, p, s], recv_sem=ag_rsem.at[way, p, s],
            device_id=there(way), device_id_type=MESH)

    def ring_recv(p, way, s):
        pltpu.make_async_copy(ag.at[p, 0], ag.at[p, 0], ag_rsem.at[way, p, s]).wait()

    def ring_step(p, s):
        if s == 0:
            local(p).wait()
        for way in (0, 1):
            if s < hops(p, way):
                if s > 0:
                    ring_recv(p, way, s - 1)
                ring(p, way, s).start()

    def weights_out():
        copies = [
            pltpu.make_async_remote_copy(
                src_ref=wg, dst_ref=wg_v.at[half_gate], send_sem=w_ssem.at[0], recv_sem=w_rsem.at[0],
                device_id={"rep": o}, device_id_type=MESH),
            pltpu.make_async_remote_copy(
                src_ref=wu, dst_ref=wu_v.at[half_gate], send_sem=w_ssem.at[1], recv_sem=w_rsem.at[1],
                device_id={"rep": o}, device_id_type=MESH),
        ]
        for q in range(HALF):
            copies.append(pltpu.make_async_remote_copy(
                src_ref=wd.at[:, pl.ds(q * w, w)], dst_ref=wd_v.at[q, half_down],
                send_sem=w_ssem.at[2 + q], recv_sem=w_rsem.at[2 + q],
                device_id={"rep": o}, device_id_type=MESH))
        return copies

    def tables():
        pltpu.make_async_copy(
            meta_v.at[pl.ds(0, zn - 1)], meta_v.at[pl.ds(0, zn - 1)], m_rsem).wait()
        row = lax.broadcasted_iota(jnp.int32, (lanes, lanes), 0)
        col = lax.broadcasted_iota(jnp.int32, (lanes, lanes), 1)
        before = ((row < col) & (row // tn == col // tn)).astype(F32).astype(BF16)
        mine = (lax.broadcasted_iota(jnp.int32, (en, lanes), 0) + en * z).astype(F32)
        sub = lax.broadcasted_iota(jnp.int32, (rows, lanes), 0)
        lane = lax.broadcasted_iota(jnp.int32, (rows, lanes), 1)
        want = (sub // zn).astype(F32)
        for h in range(zn // per):
            both = meta_v[h * per]
            for b in range(1, per):
                both = both + meta_v[h * per + b]
            named = jnp.zeros((en, lanes), F32)
            prob = jnp.zeros((en, lanes), F32)
            for k in range(8):
                hit = both[k:k + 1, :] == mine
                named = named + jnp.where(hit, 1.0, 0.0)
                prob = prob + jnp.where(hit, both[8 + k:9 + k, :], 0.0)
            rank = dot(named.astype(BF16), before, NN)
            rank_v[h] = jnp.where(named > 0.0, rank, -1.0)
            prob_v[h] = prob
            here = (sub % zn) == (h * per + lane // tn)
            for e in range(en):
                hit = (rank_v[h, e:e + 1, :] == want) & here
                at = (slice(e * rows, (e + 1) * rows), slice(h * lanes, (h + 1) * lanes))
                pick_f[at] = jnp.where(hit, 1.0, 0.0)
                prob_f[at] = jnp.where(hit, prob_v[h, e:e + 1, :], 0.0)
        pick_b[...] = pick_f[...].astype(BF16)

    def select(p):
        x = ag[p].reshape(zn * tn, w)
        got = dot(pick_b[...], x, NN)
        if p >= HALF:
            got = got * jnp.sum(prob_f[...], axis=1, keepdims=True)
        send[p] = got.reshape(slots // 8, 8, w).astype(BF16).reshape(en, rows // 8, 8, w)

    def fan_out(src, dst, p, ssem, rsem, osem):
        pltpu.make_async_copy(src.at[p, c], dst.at[p, c], osem.at[p]).start()

        def one(d, carry):
            to = lax.rem(c + d, en)
            pltpu.make_async_remote_copy(
                src_ref=src.at[p, to], dst_ref=dst.at[p, c], send_sem=ssem.at[p], recv_sem=rsem.at[p],
                device_id={"exp": to}, device_id_type=MESH).start()
            return carry

        lax.fori_loop(1, en, one, 0)

    def fan_wait(buf, p, sem):
        pltpu.make_async_copy(
            buf.at[p, pl.ds(0, en - 1)], buf.at[p, pl.ds(0, en - 1)], sem.at[p]).wait()

    def fan_recv(dst, p, rsem, osem):
        fan_wait(dst, p, rsem)
        pltpu.make_async_copy(dst.at[p, 0], dst.at[p, 0], osem.at[p]).wait()

    def flat(ref, p):
        return ref[p].astype(F32).reshape(slots, w).astype(BF16)

    for t in range(PIECES + long):
        if t < PIECES:
            ring_step(t, 0)
        for s in range(1, long):
            if 0 <= t - s < PIECES:
                ring_step(t - s, s)
        if t == 0:
            for copy in weights_out():
                copy.start()
            tables()
        p = t - long
        if 0 <= p < PIECES:
            for way in (0, 1):
                if hops(p, way) > 0:
                    ring_recv(p, way, hops(p, way) - 1)
            select(p)
            fan_out(send, recv, p, d_ssem, d_rsem, own_sem)

    pick_t[...] = pick_f[...].T.astype(BF16)
    prob_t = prob_f[...].T
    hi_t[...] = prob_t.astype(BF16)
    lo_t[...] = (prob_t - prob_t.astype(BF16).astype(F32)).astype(BF16)

    for copy in w_local:
        copy.wait()
    for copy in weights_out():
        copy.wait_recv()

    gate[...] = jnp.zeros_like(gate)
    up[...] = jnp.zeros_like(up)
    dh[...] = jnp.zeros_like(dh)

    def take_tokens(p, carry):
        fan_recv(recv, p, d_rsem, own_sem)
        x = flat(recv, p)
        gate[...] += dot(x, wg_v[p], NN)
        up[...] += dot(x, wu_v[p], NN)
        return carry

    lax.fori_loop(0, HALF, take_tokens, 0)
    chunk = slots // 8

    def forward(i, carry):
        at = pl.ds(pl.multiple_of(i * chunk, chunk), chunk)
        g = gate[at, :]
        hid[at, :] = (g * jax.nn.sigmoid(g) * up[at, :]).astype(BF16)
        return carry

    lax.fori_loop(0, 8, forward, 0)

    def give_out(p, carry):
        y = dot(hid[...], wd_v[p], NN)
        back[p] = y.reshape(slots // 8, 8, w).astype(BF16).reshape(en, rows // 8, 8, w)
        fan_out(back, ret, p, b_ssem, b_rsem, bown_sem)
        return carry

    lax.fori_loop(0, HALF, give_out, 0)

    def take_cot(q, carry):
        p = q + HALF
        fan_recv(recv, p, d_rsem, own_sem)
        dh[...] += dot(flat(recv, p), wd_v[q], NT)
        return carry

    lax.fori_loop(0, HALF, take_cot, 0)

    def backward(i, carry):
        at = pl.ds(pl.multiple_of(i * chunk, chunk), chunk)
        g = gate[at, :]
        sig = jax.nn.sigmoid(g)
        d = dh[at, :]
        dgu[at, :ff] = (d * up[at, :] * sig * (1.0 + g * (1.0 - sig))).astype(BF16)
        dgu[at, ff:] = (d * (g * sig)).astype(BF16)
        return carry

    lax.fori_loop(0, 8, backward, 0)

    def give_grad(q, carry):
        p = q + HALF
        x = dot(dgu[:, :ff], wg_v[q], NT) + dot(dgu[:, ff:], wu_v[q], NT)
        back[p] = x.reshape(slots // 8, 8, w).astype(BF16).reshape(en, rows // 8, 8, w)
        fan_out(back, ret, p, b_ssem, b_rsem, bown_sem)
        return carry

    lax.fori_loop(0, HALF, give_grad, 0)

    def partial_gu(dst, half):
        def one(i, carry):
            dst[i] = dot(flat(recv, half * wq + i), dgu[...], TN).astype(BF16)
            return carry

        lax.fori_loop(0, wq, one, 0)

    def partial_d(dst, half):
        def one(q, carry):
            part_hid = hid[:, pl.ds(pl.multiple_of(half * fh, fh), fh)]
            dst[q] = dot(part_hid, flat(recv, q + HALF), TN).astype(BF16)
            return carry

        lax.fori_loop(0, HALF, one, 0)

    def grads_out():
        return [
            pltpu.make_async_remote_copy(
                src_ref=snd_gu, dst_ref=rcv_gu, send_sem=g_ssem.at[0], recv_sem=g_rsem.at[0],
                device_id={"rep": o}, device_id_type=MESH),
            pltpu.make_async_remote_copy(
                src_ref=snd_d, dst_ref=rcv_d, send_sem=g_ssem.at[1], recv_sem=g_rsem.at[1],
                device_id={"rep": o}, device_id_type=MESH),
        ]

    partial_gu(snd_gu, o)
    grads_out()[0].start()
    partial_d(snd_d, o)
    grads_out()[1].start()
    partial_gu(own_gu, r)
    partial_d(own_d, r)

    def combine(p):
        fan_recv(ret, p, b_rsem, bown_sem)
        x = flat(ret, p)
        if p < HALF:
            total = dot(hi_t[...], x, NN) + dot(lo_t[...], x, NN)
        else:
            total = dot(pick_t[...], x, NN)
        part[p] = total.reshape(zn, tn, w)

    def rs_send(p, way, s):
        return pltpu.make_async_remote_copy(
            src_ref=rs_s.at[way, p, s], dst_ref=rs_r.at[way, p, s],
            send_sem=rs_ssem.at[way, p, s], recv_sem=rs_rsem.at[way, p, s],
            device_id=there(way), device_id_type=MESH)

    def rs_step(p, s):
        for way in (0, 1):
            n = hops(p, way)
            if s < n:
                block = lax.rem(z + step(way) * (n - s) + zn, zn)
                value = part[p, block]
                if s > 0:
                    rs_send(p, way, s - 1).wait_recv()
                    value = value + rs_r[way, p, s - 1].astype(F32)
                rs_s[way, p, s] = value.astype(BF16)
                rs_send(p, way, s).start()

    def rs_final(p):
        value = part[p, z]
        for way in (0, 1):
            n = hops(p, way)
            if n > 0:
                rs_send(p, way, n - 1).wait_recv()
                value = value + rs_r[way, p, n - 1].astype(F32)
        dst = y_v if p < HALF else dx_v
        q = p % HALF
        dst[:, q * w:(q + 1) * w] = value.astype(BF16)

    def finish_gu(i, carry):
        own_gu[i] = (own_gu[i].astype(F32) + rcv_gu[i].astype(F32)).astype(BF16)
        return carry

    def finish_d(i, carry):
        own_d[i] = (own_d[i].astype(F32) + rcv_d[i].astype(F32)).astype(BF16)
        return carry

    def results():
        copies = [
            pltpu.make_async_copy(own_gu.at[:, :, pl.ds(0, ff)], out_g, o_sem.at[0]),
            pltpu.make_async_copy(own_gu.at[:, :, pl.ds(ff, ff)], out_u, o_sem.at[1]),
        ]
        for q in range(HALF):
            copies.append(pltpu.make_async_copy(
                own_d.at[q], out_d.at[:, pl.ds(q * w, w)], o_sem.at[2 + q]))
        return copies

    for t in range(PIECES + long + 1):
        if t < PIECES:
            combine(t)
            rs_step(t, 0)
        for s in range(1, long):
            if 0 <= t - s < PIECES:
                rs_step(t - s, s)
        if 0 <= t - long < PIECES:
            rs_final(t - long)
        if t == HALF - 1:
            for copy in grads_out():
                copy.wait_recv()
            lax.fori_loop(0, wq, finish_gu, 0)
            lax.fori_loop(0, HALF, finish_d, 0)
            for copy in results():
                copy.start()

    last = [
        pltpu.make_async_copy(y_v, out_y, o_sem.at[2 + HALF]),
        pltpu.make_async_copy(dx_v, out_dx, o_sem.at[3 + HALF]),
    ]
    for copy in last:
        copy.start()

    pltpu.make_async_copy(meta_v.at[pl.ds(0, zn - 1)], meta_v.at[pl.ds(0, zn - 1)], m_ssem).wait()
    for copy in weights_out() + grads_out():
        copy.wait_send()
    for p in range(PIECES):
        for way in (0, 1):
            for s in range(hops(p, way)):
                ring(p, way, s).wait_send()
                rs_send(p, way, s).wait_send()
        fan_wait(send, p, d_ssem)
        fan_wait(back, p, b_ssem)
    for copy in results() + last:
        copy.wait()


def local(zn, en, tokens, cotangent, expert_ids, gate_probs, gate_weight, up_weight, down_weight):
    tn, d = tokens.shape
    ff = gate_weight.shape[2]
    w = d // HALF
    wq = HALF // 2
    fh = ff // 2
    rows = RANKS * zn
    slots = en * rows
    lanes = 128
    per = lanes // tn
    long = zn // 2
    z = lax.axis_index("grp")
    table = jnp.concatenate([expert_ids.astype(F32), gate_probs], axis=1).T
    spot = jnp.arange(lanes, dtype=jnp.int32)[None, :] // tn == lax.rem(z, per)
    meta = jnp.where(spot, jnp.tile(table, (1, per)), 0.0)
    vm = pltpu.VMEM
    dma = pltpu.SemaphoreType.DMA
    group = (PIECES, en, rows // 8, 8, w)
    scratch = [
        vm((PIECES, zn, tn, w), BF16),
        vm((zn, 16, lanes), F32),
        vm((HALF, w, ff), BF16),
        vm((HALF, w, ff), BF16),
        vm((HALF, ff, w), BF16),
        vm((zn // per, en, lanes), F32),
        vm((zn // per, en, lanes), F32),
        vm((slots, zn * tn), F32),
        vm((slots, zn * tn), F32),
        vm((slots, zn * tn), BF16),
        vm((zn * tn, slots), BF16),
        vm((zn * tn, slots), BF16),
        vm((zn * tn, slots), BF16),
        vm(group, BF16),
        vm(group, BF16),
        vm((slots, ff), F32),
        vm((slots, ff), F32),
        vm((slots, ff), F32),
        vm((slots, ff), BF16),
        vm((slots, 2 * ff), BF16),
        vm(group, BF16),
        vm(group, BF16),
        vm((PIECES, zn, tn, w), F32),
        vm((2, PIECES, long, tn, w), BF16),
        vm((2, PIECES, long, tn, w), BF16),
        vm((wq, w, 2 * ff), BF16),
        vm((HALF, fh, w), BF16),
        vm((wq, w, 2 * ff), BF16),
        vm((HALF, fh, w), BF16),
        vm((wq, w, 2 * ff), BF16),
        vm((HALF, fh, w), BF16),
        vm((tn, d), BF16),
        vm((tn, d), BF16),
        dma((PIECES,)), dma, dma((2 + HALF,)), dma, dma, dma((2 + HALF,)), dma((2 + HALF,)),
        dma((2, PIECES, long)), dma((2, PIECES, long)), dma((PIECES,)), dma((PIECES,)), dma((PIECES,)),
        dma((PIECES,)), dma((PIECES,)), dma((PIECES,)), dma((2, PIECES, long)), dma((2, PIECES, long)),
        dma((2,)), dma((2,)), dma((4 + HALF,)),
    ]
    hbm = pl.BlockSpec(memory_space=pl.ANY)
    y, dx, g, u, dd = pl.pallas_call(
        functools.partial(kernel, zn, en),
        out_shape=(
            jax.ShapeDtypeStruct((tn, d), BF16),
            jax.ShapeDtypeStruct((tn, d), BF16),
            jax.ShapeDtypeStruct((wq, w, ff), BF16),
            jax.ShapeDtypeStruct((wq, w, ff), BF16),
            jax.ShapeDtypeStruct((fh, d), BF16),
        ),
        in_specs=[hbm] * 6,
        out_specs=(hbm,) * 5,
        scratch_shapes=scratch,
        name="moe",
        compiler_params=pltpu.CompilerParams(
            collective_id=0, has_side_effects=True, vmem_limit_bytes=67043328),
    )(
        tokens, cotangent, meta,
        gate_weight.reshape(wq, w, ff), up_weight.reshape(wq, w, ff), down_weight.reshape(fh, d),
    )
    return y, dx, g.reshape(1, wq * w, ff), u.reshape(1, wq * w, ff), dd.reshape(1, fh, d)


def solution(mesh):
    tokens = P(("grp", "exp", "rep"), None)
    weight = P(("grp", "exp"), "rep", None)
    return jax.shard_map(
        functools.partial(local, mesh.shape["grp"], mesh.shape["exp"]),
        mesh=mesh,
        in_specs=(tokens,) * 4 + (weight,) * 3,
        out_specs=(tokens,) * 2 + (weight,) * 3,
        check_vma=False,
    )
```

time: 307 us -> 134 us (0.44)
  waiting for transfers between devices: 170 us -> 0 us
  Pallas kernels: 0 us -> 122 us
  matrix products: 34.4 us -> 0 us
  starting transfers between devices: 33.1 us -> 0 us
  local copies, waits for them, and re-layouts: 39.7 us -> 9.12 us
  between operations: 14.4 us -> 0.66 us
  other arithmetic: 14.2 us -> 1.99 us
    all_to_all x3 -> x0, waiting for transfers between devices: 168 us -> none  [the longest x1 78.8 us: side_by_side(): lax.all_to_all(both, axis, split_axis=split_dim, concat_axis=concat_dim,...]
    pallas_call x0 -> x1, Pallas kernels: none -> 122 us  [local(): pl.pallas_call(functools.partial(kernel, zn, en), out_shape=(jax.ShapeDty...]
    dot_general x18 -> x0, matrix products: 34.4 us -> none  [the longest x3 8.9 us: contract_cols(): lax.dot_general(left, right, (((1,), (1,)), ((), ())), preferred_element_...]
    all_to_all x3 -> x0, starting transfers between devices: 31.1 us -> none  [the longest x1 15.4 us: local(): lax.all_to_all(send_tokens.reshape(expert_count, capacity, model_width),...]
    reshape x10 -> x0, local copies, waits for them, and re-layouts: 30.8 us -> none  [the longest x1 5.17 us: local(): send_scaled.reshape(expert_count, capacity, model_width)]
    concatenate x2 -> x0, other arithmetic: 9.06 us -> none  [the longest x1 4.76 us: side_by_side(): both = jnp.concatenate(arrays, axis=along)]
    unnamed x36 -> x9, local copies, waits for them, and re-layouts: 1.92 us -> 9.03 us
    split x1 -> x0, local copies, waits for them, and re-layouts: 6.79 us -> none  [side_by_side(): jnp.split(lax.all_to_all(both, axis, split_axis=split_dim, concat_axis=co...]
  transfers between devices with their start and end apart: 10 -> 0, of which waited for: 4 -> 0; matrix products, arithmetic and copies ran while one was open for 13% -> 0% of each run, Pallas kernels for 0% -> 0%
where the time goes in v1:
time: 134 us
  Pallas kernels  122 us (91%)
  local copies, waits for them, and re-layouts  9.12 us (7%)
  other arithmetic  1.99 us (1%)
    pallas_call x1, Pallas kernels, local(): pl.pallas_call(functools.partial(kernel, zn, en), out_shape=(jax.ShapeDty...  122 us
    unnamed x9, local copies, waits for them, and re-layouts  9.03 us

profile of v1, /device:TPU:2, one launch (start us, length us, event | category | flops | bytes accessed | tf_op | source)
XLA Modules:
  0.0 133.9 jit_solution(14989508499662282584)
XLA Ops:
  0.6 0.7 convert_element_type.3
  1.3 0.7 maximum_bitcast_fusion
  2.0 0.1 tile.10
  2.1 0.6 broadcast_select_fusion.meta
  2.7 122.1 %moe.1 = (bf16[32,2048]{1,0:T(8,128)(2,1)}, bf16[32,2048]{1,0:T(8,128)(2,1)}, bf16[2,512,768]{2,1,0:T(8,128)(2,1)}, bf16[2,512,768]{2,1,0:T(8,128)(2,1)}, bf16[384,2048]{1,0:T(8,128)(2,1)}) custom-call(bf16[32,2048]{1,0:T(8,128)(2,1)} %tok.1, bf16[32,2048]{1,0:T(8,128)(2,1)} %cot.1, f32[16,128]{1,0:T(8,128)} %broadcast_select_fusion.meta, ...), custom_call_target="tpu_custom_call" | custom-call | tf_op jit(solution)/shard_map/moe/pallas_call | solution.py:473
  124.8 1.6 %copy.17 = bf16[32,2048]{1,0:T(8,128)(2,1)} copy(bf16[32,2048]{1,0:T(8,128)(2,1)} %get-tuple-element.20) | data formatting | bytes 262144
  126.4 1.6 %copy.18 = bf16[32,2048]{1,0:T(8,128)(2,1)} copy(bf16[32,2048]{1,0:T(8,128)(2,1)} %get-tuple-element.21) | data formatting | bytes 262144
  128.0 0.0 copy-start.1
  128.0 2.8 %copy.19 = bf16[1,1024,768]{2,1,0:T(8,128)(2,1)} copy(bf16[1,1024,768]{2,1,0:T(8,128)(2,1)} %bitcast.13) | data formatting | bytes 3145728
  130.7 0.0 copy-done.1
  130.8 0.0 copy-start
  130.8 1.1 copy.20
  131.9 0.8 copy-done
  132.7 1.1 copy.21
  (2 shorter events, 0.0 us)
Async XLA Ops:
  128.0 2.8 %copy-start.1 = (bf16[2,512,768]{2,1,0:T(8,128)(2,1)S(1)}, bf16[2,512,768]{2,1,0:T(8,128)(2,1)}, u32[]{:S(2)}) copy-start(bf16[2,512,768]{2,1,0:T(8,128)(2,1)} %get-tuple-element.13) | copy-start | bytes 4718596
  130.8 2.0 %copy-start = (bf16[384,2048]{1,0:T(8,128)(2,1)S(1)}, bf16[384,2048]{1,0:T(8,128)(2,1)}, u32[]{:S(2)}) copy-start(bf16[384,2048]{1,0:T(8,128)(2,1)} %get-tuple-element.14) | copy-start | bytes 4718596

commit v2 on v1

--- a/solution.py
+++ b/solution.py
@@ -26,13 +26,12 @@
 
 def kernel(
     zn, en,
-    tok, cot, meta, wg, wu, wd,
+    ids, prob, tok, cot, wg, wu, wd,
     out_y, out_dx, out_g, out_u, out_d,
     ag, meta_v, wg_v, wu_v, wd_v, rank_v, prob_v, pick_f, prob_f, pick_b, pick_t, hi_t, lo_t,
-    send, recv, gate, up, dh, hid, dgu, back, ret, part, rs_s, rs_r, own_gu, own_d, snd_gu, snd_d,
-    rcv_gu, rcv_d, y_v, dx_v,
-    l_sem, lm_sem, lw_sem, m_ssem, m_rsem, w_ssem, w_rsem, ag_ssem, ag_rsem, d_ssem, d_rsem, own_sem,
-    b_ssem, b_rsem, bown_sem, rs_ssem, rs_rsem, g_ssem, g_rsem, o_sem,
+    send, recv, gate, up, dh, hid, dgu, back, ret, part, rs_s, rs_r, snd_gu, snd_d, rcv_gu, rcv_d,
+    l_sem, lw_sem, m_ssem, m_rsem, w_ssem, w_rsem, ag_ssem, ag_rsem, d_ssem, d_rsem, own_sem,
+    b_ssem, b_rsem, bown_sem, rs_ssem, rs_rsem, g_ssem, g_rsem,
 ):
     z = lax.axis_index("grp")
     c = lax.axis_index("exp")
@@ -57,13 +56,25 @@
     def there(way):
         return {"grp": lax.rem(z + step(way) + zn, zn)}
 
+    barrier = pltpu.get_barrier_semaphore()
+    pl.semaphore_signal(barrier, inc=1, device_id={"rep": o}, device_id_type=MESH)
+
+    def greet_grp(d, carry):
+        pl.semaphore_signal(barrier, inc=1, device_id={"grp": lax.rem(z + d, zn)}, device_id_type=MESH)
+        return carry
+
+    def greet_exp(d, carry):
+        pl.semaphore_signal(barrier, inc=1, device_id={"exp": lax.rem(c + d, en)}, device_id_type=MESH)
+        return carry
+
+    lax.fori_loop(1, zn, greet_grp, 0)
+    lax.fori_loop(1, en, greet_exp, 0)
+
     def local(p):
         src = tok if p < HALF else cot
         return pltpu.make_async_copy(
             src.at[:, pl.ds((p % HALF) * w, w)], ag.at[p, z], l_sem.at[p])
 
-    meta_in = pltpu.make_async_copy(meta, meta_v.at[z], lm_sem)
-    meta_in.start()
     for p in range(PIECES):
         local(p).start()
     wq = HALF // 2
@@ -79,22 +90,14 @@
     for copy in w_local:
         copy.start()
 
-    barrier = pltpu.get_barrier_semaphore()
-    pl.semaphore_signal(barrier, inc=1, device_id={"rep": o}, device_id_type=MESH)
-
-    def greet_grp(d, carry):
-        pl.semaphore_signal(barrier, inc=1, device_id={"grp": lax.rem(z + d, zn)}, device_id_type=MESH)
-        return carry
-
-    def greet_exp(d, carry):
-        pl.semaphore_signal(barrier, inc=1, device_id={"exp": lax.rem(c + d, en)}, device_id_type=MESH)
-        return carry
-
-    lax.fori_loop(1, zn, greet_grp, 0)
-    lax.fori_loop(1, en, greet_exp, 0)
+    lane = lax.broadcasted_iota(jnp.int32, (tn, lanes), 1)
+    token = lax.broadcasted_iota(jnp.int32, (tn, lanes), 0)
+    spot = ((lane % tn == token) & (lane // tn == lax.rem(z, per))).astype(F32)
+    for i, table in enumerate((ids[...].astype(F32), prob[...])):
+        meta_v[z, 8 * i:8 * i + 8, :] = lax.dot_general(
+            table, spot, (NN, ((), ())), precision=lax.Precision.HIGHEST, preferred_element_type=F32)
     pl.semaphore_wait(barrier, 1 + (zn - 1) + (en - 1))
 
-    meta_in.wait()
 
     def send_meta(d, carry):
         pltpu.make_async_remote_copy(
@@ -201,22 +204,20 @@
         return ref[p].astype(F32).reshape(slots, w).astype(BF16)
 
     for t in range(PIECES + long):
-        if t < PIECES:
-            ring_step(t, 0)
-        for s in range(1, long):
+        p = t - long
+        if p == 0:
+            tables()
+        if p >= 0:
+            for way in (0, 1):
+                ring_recv(p, way, hops(p, way) - 1)
+            select(p)
+            fan_out(send, recv, p, d_ssem, d_rsem, own_sem)
+        for s in range(long - 1, -1, -1):
             if 0 <= t - s < PIECES:
                 ring_step(t - s, s)
         if t == 0:
             for copy in weights_out():
                 copy.start()
-            tables()
-        p = t - long
-        if 0 <= p < PIECES:
-            for way in (0, 1):
-                if hops(p, way) > 0:
-                    ring_recv(p, way, hops(p, way) - 1)
-            select(p)
-            fan_out(send, recv, p, d_ssem, d_rsem, own_sem)
 
     pick_t[...] = pick_f[...].T.astype(BF16)
     prob_t = prob_f[...].T
@@ -286,20 +287,33 @@
 
     lax.fori_loop(0, HALF, give_grad, 0)
 
-    def partial_gu(dst, half):
-        def one(i, carry):
-            dst[i] = dot(flat(recv, half * wq + i), dgu[...], TN).astype(BF16)
-            return carry
-
-        lax.fori_loop(0, wq, one, 0)
-
-    def partial_d(dst, half):
-        def one(q, carry):
-            part_hid = hid[:, pl.ds(pl.multiple_of(half * fh, fh), fh)]
-            dst[q] = dot(part_hid, flat(recv, q + HALF), TN).astype(BF16)
-            return carry
-
-        lax.fori_loop(0, HALF, one, 0)
+    def partial_gu(i, half):
+        return dot(flat(recv, half * wq + i), dgu[...], TN).astype(BF16)
+
+    def partial_d(q, half):
+        part_hid = hid[:, pl.ds(pl.multiple_of(half * fh, fh), fh)]
+        return dot(part_hid, flat(recv, q + HALF), TN).astype(BF16)
+
+    def columns(q):
+        return pl.ds(pl.multiple_of(q * w, w), w)
+
+    def other_gu(i, carry):
+        snd_gu[i] = partial_gu(i, o)
+        return carry
+
+    def other_d(q, carry):
+        snd_d[q] = partial_d(q, o)
+        return carry
+
+    def own_gu(i, carry):
+        both = partial_gu(i, r)
+        out_g[i] = both[:, :ff]
+        out_u[i] = both[:, ff:]
+        return carry
+
+    def own_d(q, carry):
+        out_d[:, columns(q)] = partial_d(q, r)
+        return carry
 
     def grads_out():
         return [
@@ -310,13 +324,6 @@
                 src_ref=snd_d, dst_ref=rcv_d, send_sem=g_ssem.at[1], recv_sem=g_rsem.at[1],
                 device_id={"rep": o}, device_id_type=MESH),
         ]
-
-    partial_gu(snd_gu, o)
-    grads_out()[0].start()
-    partial_d(snd_d, o)
-    grads_out()[1].start()
-    partial_gu(own_gu, r)
-    partial_d(own_d, r)
 
     def combine(p):
         fan_recv(ret, p, b_rsem, bown_sem)
@@ -349,67 +356,66 @@
         value = part[p, z]
         for way in (0, 1):
             n = hops(p, way)
-            if n > 0:
-                rs_send(p, way, n - 1).wait_recv()
-                value = value + rs_r[way, p, n - 1].astype(F32)
-        dst = y_v if p < HALF else dx_v
+            rs_send(p, way, n - 1).wait_recv()
+            value = value + rs_r[way, p, n - 1].astype(F32)
+        dst = out_y if p < HALF else out_dx
         q = p % HALF
         dst[:, q * w:(q + 1) * w] = value.astype(BF16)
 
     def finish_gu(i, carry):
-        own_gu[i] = (own_gu[i].astype(F32) + rcv_gu[i].astype(F32)).astype(BF16)
-        return carry
-
-    def finish_d(i, carry):
-        own_d[i] = (own_d[i].astype(F32) + rcv_d[i].astype(F32)).astype(BF16)
-        return carry
-
-    def results():
-        copies = [
-            pltpu.make_async_copy(own_gu.at[:, :, pl.ds(0, ff)], out_g, o_sem.at[0]),
-            pltpu.make_async_copy(own_gu.at[:, :, pl.ds(ff, ff)], out_u, o_sem.at[1]),
-        ]
-        for q in range(HALF):
-            copies.append(pltpu.make_async_copy(
-                own_d.at[q], out_d.at[:, pl.ds(q * w, w)], o_sem.at[2 + q]))
-        return copies
-
-    for t in range(PIECES + long + 1):
-        if t < PIECES:
-            combine(t)
-            rs_step(t, 0)
-        for s in range(1, long):
-            if 0 <= t - s < PIECES:
-                rs_step(t - s, s)
-        if 0 <= t - long < PIECES:
-            rs_final(t - long)
-        if t == HALF - 1:
+        out_g[i] = (out_g[i].astype(F32) + rcv_gu[i, :, :ff].astype(F32)).astype(BF16)
+        out_u[i] = (out_u[i].astype(F32) + rcv_gu[i, :, ff:].astype(F32)).astype(BF16)
+        return carry
+
+    def finish_d(q, carry):
+        out_d[:, columns(q)] = (out_d[:, columns(q)].astype(F32) + rcv_d[q].astype(F32)).astype(BF16)
+        return carry
+
+    def fill(t):
+        if t < wq:
+            other_gu(t, 0)
+            if t == wq - 1:
+                grads_out()[0].start()
+        elif t == wq:
+            lax.fori_loop(0, HALF, other_d, 0)
+            grads_out()[1].start()
+        elif t < 2 * wq + 1:
+            own_gu(t - wq - 1, 0)
+        elif t == 2 * wq + 1:
+            lax.fori_loop(0, HALF, own_d, 0)
+        elif t == 2 * wq + 2:
             for copy in grads_out():
                 copy.wait_recv()
             lax.fori_loop(0, wq, finish_gu, 0)
             lax.fori_loop(0, HALF, finish_d, 0)
-            for copy in results():
-                copy.start()
-
-    last = [
-        pltpu.make_async_copy(y_v, out_y, o_sem.at[2 + HALF]),
-        pltpu.make_async_copy(dx_v, out_dx, o_sem.at[3 + HALF]),
-    ]
-    for copy in last:
-        copy.start()
-
-    pltpu.make_async_copy(meta_v.at[pl.ds(0, zn - 1)], meta_v.at[pl.ds(0, zn - 1)], m_ssem).wait()
-    for copy in weights_out() + grads_out():
-        copy.wait_send()
+        elif t == 2 * wq + 3:
+            pltpu.make_async_copy(
+                meta_v.at[pl.ds(0, zn - 1)], meta_v.at[pl.ds(0, zn - 1)], m_ssem).wait()
+            for copy in weights_out() + grads_out():
+                copy.wait_send()
+            for p in range(PIECES):
+                for way in (0, 1):
+                    for s in range(hops(p, way)):
+                        ring(p, way, s).wait_send()
+            for p in range(PIECES):
+                fan_wait(send, p, d_ssem)
+                fan_wait(back, p, b_ssem)
+
+    for t in range(PIECES + long + 1):
+        for s in range(long - 1, 0, -1):
+            if 0 <= t - s - 1 < PIECES:
+                rs_step(t - s - 1, s)
+        if t < PIECES:
+            combine(t)
+            rs_step(t, 0)
+        if t > long:
+            rs_final(t - long - 1)
+        fill(t)
+
     for p in range(PIECES):
         for way in (0, 1):
             for s in range(hops(p, way)):
-                ring(p, way, s).wait_send()
                 rs_send(p, way, s).wait_send()
-        fan_wait(send, p, d_ssem)
-        fan_wait(back, p, b_ssem)
-    for copy in results() + last:
-        copy.wait()
 
 
 def local(zn, en, tokens, cotangent, expert_ids, gate_probs, gate_weight, up_weight, down_weight):
@@ -423,10 +429,6 @@
     lanes = 128
     per = lanes // tn
     long = zn // 2
-    z = lax.axis_index("grp")
-    table = jnp.concatenate([expert_ids.astype(F32), gate_probs], axis=1).T
-    spot = jnp.arange(lanes, dtype=jnp.int32)[None, :] // tn == lax.rem(z, per)
-    meta = jnp.where(spot, jnp.tile(table, (1, per)), 0.0)
     vm = pltpu.VMEM
     dma = pltpu.SemaphoreType.DMA
     group = (PIECES, en, rows // 8, 8, w)
@@ -460,33 +462,29 @@
         vm((HALF, fh, w), BF16),
         vm((wq, w, 2 * ff), BF16),
         vm((HALF, fh, w), BF16),
-        vm((wq, w, 2 * ff), BF16),
-        vm((HALF, fh, w), BF16),
-        vm((tn, d), BF16),
-        vm((tn, d), BF16),
-        dma((PIECES,)), dma, dma((2 + HALF,)), dma, dma, dma((2 + HALF,)), dma((2 + HALF,)),
+        dma((PIECES,)), dma((2 + HALF,)), dma, dma, dma((2 + HALF,)), dma((2 + HALF,)),
         dma((2, PIECES, long)), dma((2, PIECES, long)), dma((PIECES,)), dma((PIECES,)), dma((PIECES,)),
         dma((PIECES,)), dma((PIECES,)), dma((PIECES,)), dma((2, PIECES, long)), dma((2, PIECES, long)),
-        dma((2,)), dma((2,)), dma((4 + HALF,)),
+        dma((2,)), dma((2,)),
     ]
     hbm = pl.BlockSpec(memory_space=pl.ANY)
     y, dx, g, u, dd = pl.pallas_call(
         functools.partial(kernel, zn, en),
         out_shape=(
-            jax.ShapeDtypeStruct((tn, d), BF16),
-            jax.ShapeDtypeStruct((tn, d), BF16),
-            jax.ShapeDtypeStruct((wq, w, ff), BF16),
-            jax.ShapeDtypeStruct((wq, w, ff), BF16),
-            jax.ShapeDtypeStruct((fh, d), BF16),
+            pltpu.VMEM((tn, d), BF16),
+            pltpu.VMEM((tn, d), BF16),
+            pltpu.VMEM((wq, w, ff), BF16),
+            pltpu.VMEM((wq, w, ff), BF16),
+            pltpu.VMEM((fh, d), BF16),
         ),
-        in_specs=[hbm] * 6,
-        out_specs=(hbm,) * 5,
+        in_specs=[pl.BlockSpec(memory_space=pltpu.VMEM)] * 2 + [hbm] * 5,
+        out_specs=(pl.BlockSpec(memory_space=pltpu.VMEM),) * 5,
         scratch_shapes=scratch,
         name="moe",
         compiler_params=pltpu.CompilerParams(
-            collective_id=0, has_side_effects=True, vmem_limit_bytes=67043328),
+            collective_id=0, has_side_effects=True, vmem_limit_bytes=58000000),
     )(
-        tokens, cotangent, meta,
+        expert_ids.T, gate_probs.T, tokens, cotangent,
         gate_weight.reshape(wq, w, ff), up_weight.reshape(wq, w, ff), down_weight.reshape(fh, d),
     )
     return y, dx, g.reshape(1, wq * w, ff), u.reshape(1, wq * w, ff), dd.reshape(1, fh, d)

time: 134 us -> 122 us (0.910)
  Pallas kernels: 122 us -> 116 us
  local copies, waits for them, and re-layouts: 9.12 us -> 4.74 us
  other arithmetic: 1.99 us -> 0 us
    pallas_call x1, Pallas kernels: 122 us -> 116 us  [local(): pl.pallas_call(functools.partial(kernel, zn, en), out_shape=(pltpu.VMEM((...]
    unnamed x9 -> x5, local copies, waits for them, and re-layouts: 9.03 us -> 4.74 us
where the time goes in v2:
time: 122 us; the launch traced here: 121 us
  Pallas kernels  116 us (95%)
  local copies, waits for them, and re-layouts  4.74 us (4%)
    pallas_call x1, Pallas kernels, local(): pl.pallas_call(functools.partial(kernel, zn, en), out_shape=(pltpu.VMEM((...  116 us
    unnamed x5, local copies, waits for them, and re-layouts  4.74 us

profile of v2, /device:TPU:2, one launch (start us, length us, event | category | flops | bytes accessed | tf_op | source)
XLA Modules:
  0.0 121.1 jit_solution(423420979658196992)
XLA Ops:
  0.6 115.7 %moe.1 = (bf16[32,2048]{1,0:T(8,128)(2,1)S(1)}, bf16[32,2048]{1,0:T(8,128)(2,1)S(1)}, bf16[2,512,768]{2,1,0:T(8,128)(2,1)S(1)}, bf16[2,512,768]{2,1,0:T(8,128)(2,1)S(1)}, bf16[384,2048]{1,0:T(8,128)(2,1)S(1)}) custom-call(s32[8,32]{1,0:T(8,128)} %bitcast.14, f32[8,32]{1,0:T(8,128)} %bitcast.15, bf16[32,2048]{1,0:T(8,128)(2,1)} %tok.1, bf16[32,2048]{1,0:T(8,128)(2,1)} %cot.1, ...), custom_call_target="tpu_custom_call" | custom-call | tf_op jit(solution)/shard_map/moe/pallas_call | solution.py:471
  116.3 0.7 copy.17
  117.0 0.7 copy.18
  117.7 1.1 copy.19
  118.8 1.1 copy.20
  119.9 1.1 copy.21

commit v3 on v2

--- a/solution.py
+++ b/solution.py
@@ -13,6 +13,8 @@
 RANKS = 3
 HALF = 4
 PIECES = 2 * HALF
+CROSS = 2
+RING = PIECES - CROSS
 
 
 def dot(a, b, dims):
@@ -32,6 +34,8 @@
     send, recv, gate, up, dh, hid, dgu, back, ret, part, rs_s, rs_r, snd_gu, snd_d, rcv_gu, rcv_d,
     l_sem, lw_sem, m_ssem, m_rsem, w_ssem, w_rsem, ag_ssem, ag_rsem, d_ssem, d_rsem, own_sem,
     b_ssem, b_rsem, bown_sem, rs_ssem, rs_rsem, g_ssem, g_rsem,
+    ids_v, chance_v, all_rank, all_prob, own_f, own_prob, own_pick, own_hi, own_lo, order,
+    x_r, z_s, z_r, back_z_s, back_z_r, back_x, ids_sem, x_ssem, x_rsem, x_own, z_ssem, z_rsem, bz_ssem, bz_rsem,
 ):
     z = lax.axis_index("grp")
     c = lax.axis_index("exp")
@@ -75,7 +79,13 @@
         return pltpu.make_async_copy(
             src.at[:, pl.ds((p % HALF) * w, w)], ag.at[p, z], l_sem.at[p])
 
-    for p in range(PIECES):
+    tables_in = [
+        pltpu.make_async_copy(ids, ids_v, ids_sem.at[0]),
+        pltpu.make_async_copy(prob, chance_v, ids_sem.at[1]),
+    ]
+    for copy in tables_in:
+        copy.start()
+    for p in list(range(RING, PIECES)) + list(range(RING)):
         local(p).start()
     wq = HALF // 2
     half_gate = pl.ds(r * wq, wq)
@@ -93,9 +103,37 @@
     lane = lax.broadcasted_iota(jnp.int32, (tn, lanes), 1)
     token = lax.broadcasted_iota(jnp.int32, (tn, lanes), 0)
     spot = ((lane % tn == token) & (lane // tn == lax.rem(z, per))).astype(F32)
-    for i, table in enumerate((ids[...].astype(F32), prob[...])):
+    for copy in tables_in:
+        copy.wait()
+    for i, table in enumerate((ids_v[...].astype(F32), chance_v[...])):
         meta_v[z, 8 * i:8 * i + 8, :] = lax.dot_general(
             table, spot, (NN, ((), ())), precision=lax.Precision.HIGHEST, preferred_element_type=F32)
+
+    row = lax.broadcasted_iota(jnp.int32, (lanes, lanes), 0)
+    col = lax.broadcasted_iota(jnp.int32, (lanes, lanes), 1)
+    before = ((row < col) & (row // tn == col // tn)).astype(F32).astype(BF16)
+    expert = lax.broadcasted_iota(jnp.int32, (en * zn, tn), 0).astype(F32)
+    named = jnp.zeros((en * zn, tn), F32)
+    weight = jnp.zeros((en * zn, tn), F32)
+    for k in range(8):
+        hit = ids_v[k:k + 1, :].astype(F32) == expert
+        named = named + jnp.where(hit, 1.0, 0.0)
+        weight = weight + jnp.where(hit, chance_v[k:k + 1, :], 0.0)
+    rank = dot(named.astype(BF16), before[:tn, :tn], NN)
+    all_rank[...] = jnp.where(named > 0.0, rank, -1.0)
+    all_prob[...] = weight
+    for e in range(en):
+        seen = all_rank[pl.ds(e, zn, stride=en), :]
+        worth = all_prob[pl.ds(e, zn, stride=en), :]
+        for k in range(RANKS):
+            at = slice((e * RANKS + k) * zn, (e * RANKS + k + 1) * zn)
+            own_f[at, :] = jnp.where(seen == float(k), 1.0, 0.0)
+            own_prob[at, :] = jnp.where(seen == float(k), worth, 0.0)
+    own_pick[...] = own_f[...].astype(BF16)
+    near = en * RANKS
+    row = lax.broadcasted_iota(jnp.int32, (slots, slots), 0)
+    col = lax.broadcasted_iota(jnp.int32, (slots, slots), 1)
+    order[...] = ((row // near == col % zn) & (row % near == col // zn)).astype(F32).astype(BF16)
     pl.semaphore_wait(barrier, 1 + (zn - 1) + (en - 1))
 
 
@@ -111,7 +149,7 @@
         block = lax.rem(z - step(way) * s + zn, zn)
         return pltpu.make_async_remote_copy(
             src_ref=ag.at[p, block], dst_ref=ag.at[p, block],
-            send_sem=ag_ssem.at[way, p, s], recv_sem=ag_rsem.at[way, p, s],
+            send_sem=ag_ssem.at[way], recv_sem=ag_rsem.at[way, p, s],
             device_id=there(way), device_id_type=MESH)
 
     def ring_recv(p, way, s):
@@ -125,6 +163,10 @@
                 if s > 0:
                     ring_recv(p, way, s - 1)
                 ring(p, way, s).start()
+
+    def ring_sent(sem, way):
+        some = ag.at[pl.ds(0, RING // 2), pl.ds(0, zn - 1)]
+        pltpu.make_async_copy(some, some, sem.at[way]).wait()
 
     def weights_out():
         copies = [
@@ -178,15 +220,15 @@
         got = dot(pick_b[...], x, NN)
         if p >= HALF:
             got = got * jnp.sum(prob_f[...], axis=1, keepdims=True)
-        send[p] = got.reshape(slots // 8, 8, w).astype(BF16).reshape(en, rows // 8, 8, w)
-
-    def fan_out(src, dst, p, ssem, rsem, osem):
-        pltpu.make_async_copy(src.at[p, c], dst.at[p, c], osem.at[p]).start()
+        send[p] = grouped(got)
+
+    def fan_out(src, i, dst, p, ssem, rsem, osem):
+        pltpu.make_async_copy(src.at[i, c], dst.at[p, c], osem.at[p]).start()
 
         def one(d, carry):
             to = lax.rem(c + d, en)
             pltpu.make_async_remote_copy(
-                src_ref=src.at[p, to], dst_ref=dst.at[p, c], send_sem=ssem.at[p], recv_sem=rsem.at[p],
+                src_ref=src.at[i, to], dst_ref=dst.at[p, c], send_sem=ssem.at[p], recv_sem=rsem.at[p],
                 device_id={"exp": to}, device_id_type=MESH).start()
             return carry
 
@@ -194,16 +236,40 @@
 
     def fan_wait(buf, p, sem):
         pltpu.make_async_copy(
-            buf.at[p, pl.ds(0, en - 1)], buf.at[p, pl.ds(0, en - 1)], sem.at[p]).wait()
+            buf.at[0, pl.ds(0, en - 1)], buf.at[0, pl.ds(0, en - 1)], sem.at[p]).wait()
 
     def fan_recv(dst, p, rsem, osem):
         fan_wait(dst, p, rsem)
         pltpu.make_async_copy(dst.at[p, 0], dst.at[p, 0], osem.at[p]).wait()
 
+    def grouped(value):
+        return value.reshape(slots // 8, 8, w).astype(BF16).reshape(en, rows // 8, 8, w)
+
+    def across(src, dst, i, d, ssem, rsem):
+        to = lax.rem(z + d, zn)
+        pltpu.make_async_remote_copy(
+            src_ref=src.at[i, to], dst_ref=dst.at[i, z], send_sem=ssem.at[i], recv_sem=rsem.at[i],
+            device_id={"grp": to}, device_id_type=MESH).start()
+
+    def across_wait(buf, i, sem):
+        some = buf.at[i, pl.ds(0, zn - 1)]
+        pltpu.make_async_copy(some, some, sem.at[i]).wait()
+
+    def by_group(dst, i, value):
+        dst[i] = dot(order[...], value, NN).astype(BF16).reshape(zn, near, w)
+
+    def from_groups(src, own, i):
+        src[i, z] = own[i, z]
+        return dot(order[...], src[i].reshape(slots, w), TN)
+
+    def select_own(i):
+        got = dot(own_pick[...], ag[RING + i, z], NN)
+        return got * jnp.sum(own_prob[...], axis=1, keepdims=True)
+
     def flat(ref, p):
         return ref[p].astype(F32).reshape(slots, w).astype(BF16)
 
-    for t in range(PIECES + long):
+    for t in range(RING + long):
         p = t - long
         if p == 0:
             tables()
@@ -211,18 +277,33 @@
             for way in (0, 1):
                 ring_recv(p, way, hops(p, way) - 1)
             select(p)
-            fan_out(send, recv, p, d_ssem, d_rsem, own_sem)
+            fan_out(send, p, recv, p, d_ssem, d_rsem, own_sem)
         for s in range(long - 1, -1, -1):
-            if 0 <= t - s < PIECES:
+            if 0 <= t - s < RING:
                 ring_step(t - s, s)
         if t == 0:
+            for i in range(CROSS):
+                local(RING + i).wait()
+                send[RING + i] = grouped(select_own(i))
+            for i in range(CROSS):
+                fan_out(send, RING + i, x_r, i, x_ssem, x_rsem, x_own)
             for copy in weights_out():
                 copy.start()
+        for i in range(CROSS):
+            if t == long + i:
+                fan_recv(x_r, i, x_rsem, x_own)
+                by_group(z_s, i, flat(x_r, i))
+            for d in sorted({t - long - i, zn - t + long + i}):
+                if 0 < t - long - i <= long:
+                    across(z_s, z_r, i, d, z_ssem, z_rsem)
 
     pick_t[...] = pick_f[...].T.astype(BF16)
     prob_t = prob_f[...].T
     hi_t[...] = prob_t.astype(BF16)
     lo_t[...] = (prob_t - prob_t.astype(BF16).astype(F32)).astype(BF16)
+    own_t = own_prob[...].T
+    own_hi[...] = own_t.astype(BF16)
+    own_lo[...] = (own_t - own_t.astype(BF16).astype(F32)).astype(BF16)
 
     for copy in w_local:
         copy.wait()
@@ -253,11 +334,23 @@
 
     def give_out(p, carry):
         y = dot(hid[...], wd_v[p], NN)
-        back[p] = y.reshape(slots // 8, 8, w).astype(BF16).reshape(en, rows // 8, 8, w)
-        fan_out(back, ret, p, b_ssem, b_rsem, bown_sem)
-        return carry
-
-    lax.fori_loop(0, HALF, give_out, 0)
+        back[p] = grouped(y)
+        fan_out(back, p, ret, p, b_ssem, b_rsem, bown_sem)
+        return carry
+
+    lax.fori_loop(0, HALF - CROSS, give_out, 0)
+
+    def give_across(i, carry):
+        by_group(back_z_s, i, dot(hid[...], wd_v[HALF - CROSS + i], NN).astype(BF16))
+
+        def one(d, inner):
+            across(back_z_s, back_z_r, i, d, bz_ssem, bz_rsem)
+            return inner
+
+        lax.fori_loop(1, zn, one, 0)
+        return carry
+
+    lax.fori_loop(0, CROSS, give_across, 0)
 
     def take_cot(q, carry):
         p = q + HALF
@@ -265,7 +358,16 @@
         dh[...] += dot(flat(recv, p), wd_v[q], NT)
         return carry
 
-    lax.fori_loop(0, HALF, take_cot, 0)
+    lax.fori_loop(0, HALF - CROSS, take_cot, 0)
+
+    def take_across(i, carry):
+        across_wait(z_r, i, z_rsem)
+        x = from_groups(z_r, z_s, i)
+        recv[RING + i] = grouped(x)
+        dh[...] += dot(x.astype(BF16), wd_v[HALF - CROSS + i], NT)
+        return carry
+
+    lax.fori_loop(0, CROSS, take_across, 0)
 
     def backward(i, carry):
         at = pl.ds(pl.multiple_of(i * chunk, chunk), chunk)
@@ -281,8 +383,8 @@
     def give_grad(q, carry):
         p = q + HALF
         x = dot(dgu[:, :ff], wg_v[q], NT) + dot(dgu[:, ff:], wu_v[q], NT)
-        back[p] = x.reshape(slots // 8, 8, w).astype(BF16).reshape(en, rows // 8, 8, w)
-        fan_out(back, ret, p, b_ssem, b_rsem, bown_sem)
+        back[p] = grouped(x)
+        fan_out(back, p, ret, p, b_ssem, b_rsem, bown_sem)
         return carry
 
     lax.fori_loop(0, HALF, give_grad, 0)
@@ -334,33 +436,49 @@
             total = dot(pick_t[...], x, NN)
         part[p] = total.reshape(zn, tn, w)
 
-    def rs_send(p, way, s):
+    rings = list(range(HALF - CROSS)) + list(range(HALF, PIECES))
+
+    def rs_send(n, way, s):
         return pltpu.make_async_remote_copy(
-            src_ref=rs_s.at[way, p, s], dst_ref=rs_r.at[way, p, s],
-            send_sem=rs_ssem.at[way, p, s], recv_sem=rs_rsem.at[way, p, s],
+            src_ref=rs_s.at[way, n, s], dst_ref=rs_r.at[way, n, s],
+            send_sem=rs_ssem.at[way], recv_sem=rs_rsem.at[way, n, s],
             device_id=there(way), device_id_type=MESH)
 
-    def rs_step(p, s):
+    def rs_step(n, s):
         for way in (0, 1):
-            n = hops(p, way)
-            if s < n:
-                block = lax.rem(z + step(way) * (n - s) + zn, zn)
-                value = part[p, block]
+            far = hops(n, way)
+            if s < far:
+                block = lax.rem(z + step(way) * (far - s) + zn, zn)
+                value = part[rings[n], block]
                 if s > 0:
-                    rs_send(p, way, s - 1).wait_recv()
-                    value = value + rs_r[way, p, s - 1].astype(F32)
-                rs_s[way, p, s] = value.astype(BF16)
-                rs_send(p, way, s).start()
-
-    def rs_final(p):
-        value = part[p, z]
-        for way in (0, 1):
-            n = hops(p, way)
-            rs_send(p, way, n - 1).wait_recv()
-            value = value + rs_r[way, p, n - 1].astype(F32)
+                    rs_send(n, way, s - 1).wait_recv()
+                    value = value + rs_r[way, n, s - 1].astype(F32)
+                rs_s[way, n, s] = value.astype(BF16)
+                rs_send(n, way, s).start()
+
+    def put(p, value):
         dst = out_y if p < HALF else out_dx
         q = p % HALF
         dst[:, q * w:(q + 1) * w] = value.astype(BF16)
+
+    def rs_final(n):
+        value = part[rings[n], z]
+        for way in (0, 1):
+            far = hops(n, way)
+            rs_send(n, way, far - 1).wait_recv()
+            value = value + rs_r[way, n, far - 1].astype(F32)
+        put(rings[n], value)
+
+    def turn(i):
+        across_wait(back_z_r, i, bz_rsem)
+        back_x[i] = grouped(from_groups(back_z_r, back_z_s, i))
+        fan_out(back_x, i, ret, HALF - CROSS + i, b_ssem, b_rsem, bown_sem)
+
+    def arrive(i):
+        p = HALF - CROSS + i
+        fan_recv(ret, p, b_rsem, bown_sem)
+        x = flat(ret, p)
+        put(p, dot(own_hi[...], x, NN) + dot(own_lo[...], x, NN))
 
     def finish_gu(i, carry):
         out_g[i] = (out_g[i].astype(F32) + rcv_gu[i, :, :ff].astype(F32)).astype(BF16)
@@ -393,29 +511,34 @@
                 meta_v.at[pl.ds(0, zn - 1)], meta_v.at[pl.ds(0, zn - 1)], m_ssem).wait()
             for copy in weights_out() + grads_out():
                 copy.wait_send()
+            for way in (0, 1):
+                ring_sent(ag_ssem, way)
+            for p in range(RING):
+                fan_wait(send, p, d_ssem)
             for p in range(PIECES):
-                for way in (0, 1):
-                    for s in range(hops(p, way)):
-                        ring(p, way, s).wait_send()
-            for p in range(PIECES):
-                fan_wait(send, p, d_ssem)
                 fan_wait(back, p, b_ssem)
-
-    for t in range(PIECES + long + 1):
+            for i in range(CROSS):
+                fan_wait(send, i, x_ssem)
+                across_wait(z_s, i, z_ssem)
+                across_wait(back_z_s, i, bz_ssem)
+
+    for t in range(RING + long + 1):
         for s in range(long - 1, 0, -1):
-            if 0 <= t - s - 1 < PIECES:
+            if 0 <= t - s - 1 < RING:
                 rs_step(t - s - 1, s)
-        if t < PIECES:
-            combine(t)
+        if t < RING:
+            combine(rings[t])
             rs_step(t, 0)
         if t > long:
             rs_final(t - long - 1)
         fill(t)
-
-    for p in range(PIECES):
-        for way in (0, 1):
-            for s in range(hops(p, way)):
-                rs_send(p, way, s).wait_send()
+        if 0 < t <= CROSS:
+            turn(t - 1)
+        if RING < t <= RING + CROSS:
+            arrive(t - RING - 1)
+
+    for way in (0, 1):
+        ring_sent(rs_ssem, way)
 
 
 def local(zn, en, tokens, cotangent, expert_ids, gate_probs, gate_weight, up_weight, down_weight):
@@ -456,16 +579,34 @@
         vm(group, BF16),
         vm(group, BF16),
         vm((PIECES, zn, tn, w), F32),
-        vm((2, PIECES, long, tn, w), BF16),
-        vm((2, PIECES, long, tn, w), BF16),
+        vm((2, RING, long, tn, w), BF16),
+        vm((2, RING, long, tn, w), BF16),
         vm((wq, w, 2 * ff), BF16),
         vm((HALF, fh, w), BF16),
         vm((wq, w, 2 * ff), BF16),
         vm((HALF, fh, w), BF16),
         dma((PIECES,)), dma((2 + HALF,)), dma, dma, dma((2 + HALF,)), dma((2 + HALF,)),
-        dma((2, PIECES, long)), dma((2, PIECES, long)), dma((PIECES,)), dma((PIECES,)), dma((PIECES,)),
-        dma((PIECES,)), dma((PIECES,)), dma((PIECES,)), dma((2, PIECES, long)), dma((2, PIECES, long)),
+        dma((2,)), dma((2, RING, long)), dma((RING,)), dma((RING,)), dma((RING,)),
+        dma((PIECES,)), dma((PIECES,)), dma((PIECES,)), dma((2,)), dma((2, RING, long)),
         dma((2,)), dma((2,)),
+        vm((8, tn), jnp.int32),
+        vm((8, tn), F32),
+        vm((en * zn, tn), F32),
+        vm((en * zn, tn), F32),
+        vm((slots, tn), F32),
+        vm((slots, tn), F32),
+        vm((slots, tn), BF16),
+        vm((tn, slots), BF16),
+        vm((tn, slots), BF16),
+        vm((slots, slots), BF16),
+        vm((CROSS,) + group[1:], BF16),
+        vm((CROSS, zn, en * RANKS, w), BF16),
+        vm((CROSS, zn, en * RANKS, w), BF16),
+        vm((CROSS, zn, en * RANKS, w), BF16),
+        vm((CROSS, zn, en * RANKS, w), BF16),
+        vm((CROSS,) + group[1:], BF16),
+        dma((2,)), dma((CROSS,)), dma((CROSS,)), dma((CROSS,)), dma((CROSS,)), dma((CROSS,)),
+        dma((CROSS,)), dma((CROSS,)),
     ]
     hbm = pl.BlockSpec(memory_space=pl.ANY)
     y, dx, g, u, dd = pl.pallas_call(
@@ -477,7 +618,7 @@
             pltpu.VMEM((wq, w, ff), BF16),
             pltpu.VMEM((fh, d), BF16),
         ),
-        in_specs=[pl.BlockSpec(memory_space=pltpu.VMEM)] * 2 + [hbm] * 5,
+        in_specs=[hbm] * 7,
         out_specs=(pl.BlockSpec(memory_space=pltpu.VMEM),) * 5,
         scratch_shapes=scratch,
         name="moe",

time: 122 us -> 109 us (0.89)
  Pallas kernels: 116 us -> 103 us
    pallas_call x1, Pallas kernels: 116 us -> 103 us  [local(): pl.pallas_call(functools.partial(kernel, zn, en), out_shape=(pltpu.VMEM((...]
where the time goes in v3:
time: 109 us; the launch traced here: 108 us
  Pallas kernels  103 us (94%)
  local copies, waits for them, and re-layouts  4.74 us (4%)
    pallas_call x1, Pallas kernels, local(): pl.pallas_call(functools.partial(kernel, zn, en), out_shape=(pltpu.VMEM((...  103 us
    unnamed x5, local copies, waits for them, and re-layouts  4.74 us

profile of v3, /device:TPU:2, one launch (start us, length us, event | category | flops | bytes accessed | tf_op | source)
XLA Modules:
  0.0 108.5 jit_solution(5516728424089227201)
XLA Ops:
  0.6 103.1 %moe.1 = (bf16[32,2048]{1,0:T(8,128)(2,1)S(1)}, bf16[32,2048]{1,0:T(8,128)(2,1)S(1)}, bf16[2,512,768]{2,1,0:T(8,128)(2,1)S(1)}, bf16[2,512,768]{2,1,0:T(8,128)(2,1)S(1)}, bf16[384,2048]{1,0:T(8,128)(2,1)S(1)}) custom-call(s32[8,32]{1,0:T(8,128)} %bitcast.14, f32[8,32]{1,0:T(8,128)} %bitcast.15, bf16[32,2048]{1,0:T(8,128)(2,1)} %tok.1, bf16[32,2048]{1,0:T(8,128)(2,1)} %cot.1, ...), custom_call_target="tpu_custom_call" | custom-call | tf_op jit(solution)/shard_map/moe/pallas_call | solution.py:612
  103.7 0.7 copy.17
  104.4 0.7 copy.18
  105.0 1.1 %copy.19 = bf16[1,1024,768]{2,1,0:T(8,128)(2,1)} copy(bf16[1,1024,768]{2,1,0:T(8,128)(2,1)S(1)} %bitcast.10) | data formatting | bytes 3145728
  106.2 1.1 %copy.20 = bf16[1,1024,768]{2,1,0:T(8,128)(2,1)} copy(bf16[1,1024,768]{2,1,0:T(8,128)(2,1)S(1)} %bitcast.9) | data formatting | bytes 3145728
  107.3 1.1 %copy.21 = bf16[1,384,2048]{2,1,0:T(8,128)(2,1)} copy(bf16[1,384,2048]{2,1,0:T(8,128)(2,1)S(1)} %bitcast.8) | data formatting | bytes 3145728

commit v4 on v3

--- a/solution.py
+++ b/solution.py
@@ -15,6 +15,8 @@
 PIECES = 2 * HALF
 CROSS = 2
 RING = PIECES - CROSS
+BACK = 2
+HOME = PIECES - BACK
 
 
 def dot(a, b, dims):
@@ -269,15 +271,61 @@
     def flat(ref, p):
         return ref[p].astype(F32).reshape(slots, w).astype(BF16)
 
+    def take_tokens(p, carry):
+        fan_recv(recv, p, d_rsem, own_sem)
+        x = flat(recv, p)
+        gate[...] += dot(x, wg_v[p], NN)
+        up[...] += dot(x, wu_v[p], NN)
+        return carry
+
+    chunk = slots // 8
+
+    def forward(i, carry):
+        at = pl.ds(pl.multiple_of(i * chunk, chunk), chunk)
+        g = gate[at, :]
+        hid[at, :] = (g * jax.nn.sigmoid(g) * up[at, :]).astype(BF16)
+        return carry
+
+
+    def give_out(p, carry):
+        y = dot(hid[...], wd_v[p], NN)
+        back[p] = grouped(y)
+        fan_out(back, p, ret, p, b_ssem, b_rsem, bown_sem)
+        return carry
+
+
+    def give_across(i, carry):
+        by_group(back_z_s, i, dot(hid[...], wd_v[HALF - BACK + i], NN).astype(BF16))
+
+        def one(d, inner):
+            across(back_z_s, back_z_r, i, d, bz_ssem, bz_rsem)
+            return inner
+
+        lax.fori_loop(1, zn, one, 0)
+        return carry
+
+
+    def deliver(p):
+        for way in (0, 1):
+            ring_recv(p, way, hops(p, way) - 1)
+        select(p)
+        fan_out(send, p, recv, p, d_ssem, d_rsem, own_sem)
+
+    def cross_on(t):
+        for i in range(CROSS):
+            far = t - long - 1 - i
+            if far == -1:
+                fan_recv(x_r, i, x_rsem, x_own)
+                by_group(z_s, i, flat(x_r, i))
+            if 0 < far <= long:
+                for d in sorted({far, zn - far}):
+                    across(z_s, z_r, i, d, z_ssem, z_rsem)
+
     for t in range(RING + long):
         p = t - long
         if p == 0:
             tables()
-        if p >= 0:
-            for way in (0, 1):
-                ring_recv(p, way, hops(p, way) - 1)
-            select(p)
-            fan_out(send, p, recv, p, d_ssem, d_rsem, own_sem)
+            deliver(p)
         for s in range(long - 1, -1, -1):
             if 0 <= t - s < RING:
                 ring_step(t - s, s)
@@ -289,13 +337,23 @@
                 fan_out(send, RING + i, x_r, i, x_ssem, x_rsem, x_own)
             for copy in weights_out():
                 copy.start()
-        for i in range(CROSS):
-            if t == long + i:
-                fan_recv(x_r, i, x_rsem, x_own)
-                by_group(z_s, i, flat(x_r, i))
-            for d in sorted({t - long - i, zn - t + long + i}):
-                if 0 < t - long - i <= long:
-                    across(z_s, z_r, i, d, z_ssem, z_rsem)
+        if p > 0:
+            deliver(p)
+        cross_on(t)
+        if p == RING - 2:
+            gate[...] = jnp.zeros_like(gate)
+            up[...] = jnp.zeros_like(up)
+            dh[...] = jnp.zeros_like(dh)
+            for copy in w_local:
+                copy.wait()
+            for copy in weights_out():
+                copy.wait_recv()
+            lax.fori_loop(0, HALF - 1, take_tokens, 0)
+    for t in range(RING + long, RING + long + CROSS):
+        cross_on(t)
+    lax.fori_loop(HALF - 1, HALF, take_tokens, 0)
+    lax.fori_loop(0, 8, forward, 0)
+    lax.fori_loop(0, BACK, give_across, 0)
 
     pick_t[...] = pick_f[...].T.astype(BF16)
     prob_t = prob_f[...].T
@@ -305,60 +363,12 @@
     own_hi[...] = own_t.astype(BF16)
     own_lo[...] = (own_t - own_t.astype(BF16).astype(F32)).astype(BF16)
 
-    for copy in w_local:
-        copy.wait()
-    for copy in weights_out():
-        copy.wait_recv()
-
-    gate[...] = jnp.zeros_like(gate)
-    up[...] = jnp.zeros_like(up)
-    dh[...] = jnp.zeros_like(dh)
-
-    def take_tokens(p, carry):
-        fan_recv(recv, p, d_rsem, own_sem)
-        x = flat(recv, p)
-        gate[...] += dot(x, wg_v[p], NN)
-        up[...] += dot(x, wu_v[p], NN)
-        return carry
-
-    lax.fori_loop(0, HALF, take_tokens, 0)
-    chunk = slots // 8
-
-    def forward(i, carry):
-        at = pl.ds(pl.multiple_of(i * chunk, chunk), chunk)
-        g = gate[at, :]
-        hid[at, :] = (g * jax.nn.sigmoid(g) * up[at, :]).astype(BF16)
-        return carry
-
-    lax.fori_loop(0, 8, forward, 0)
-
-    def give_out(p, carry):
-        y = dot(hid[...], wd_v[p], NN)
-        back[p] = grouped(y)
-        fan_out(back, p, ret, p, b_ssem, b_rsem, bown_sem)
-        return carry
-
-    lax.fori_loop(0, HALF - CROSS, give_out, 0)
-
-    def give_across(i, carry):
-        by_group(back_z_s, i, dot(hid[...], wd_v[HALF - CROSS + i], NN).astype(BF16))
-
-        def one(d, inner):
-            across(back_z_s, back_z_r, i, d, bz_ssem, bz_rsem)
-            return inner
-
-        lax.fori_loop(1, zn, one, 0)
-        return carry
-
-    lax.fori_loop(0, CROSS, give_across, 0)
-
     def take_cot(q, carry):
         p = q + HALF
         fan_recv(recv, p, d_rsem, own_sem)
         dh[...] += dot(flat(recv, p), wd_v[q], NT)
         return carry
 
-    lax.fori_loop(0, HALF - CROSS, take_cot, 0)
 
     def take_across(i, carry):
         across_wait(z_r, i, z_rsem)
@@ -367,6 +377,9 @@
         dh[...] += dot(x.astype(BF16), wd_v[HALF - CROSS + i], NT)
         return carry
 
+    lax.fori_loop(0, HALF - CROSS - 1, take_cot, 0)
+    lax.fori_loop(0, HALF - BACK, give_out, 0)
+    lax.fori_loop(HALF - CROSS - 1, HALF - CROSS, take_cot, 0)
     lax.fori_loop(0, CROSS, take_across, 0)
 
     def backward(i, carry):
@@ -436,12 +449,12 @@
             total = dot(pick_t[...], x, NN)
         part[p] = total.reshape(zn, tn, w)
 
-    rings = list(range(HALF - CROSS)) + list(range(HALF, PIECES))
+    rings = list(range(HALF - BACK)) + list(range(HALF, PIECES))
 
     def rs_send(n, way, s):
         return pltpu.make_async_remote_copy(
             src_ref=rs_s.at[way, n, s], dst_ref=rs_r.at[way, n, s],
-            send_sem=rs_ssem.at[way], recv_sem=rs_rsem.at[way, n, s],
+            send_sem=rs_ssem.at[way, n], recv_sem=rs_rsem.at[way, n, s],
             device_id=there(way), device_id_type=MESH)
 
     def rs_step(n, s):
@@ -472,10 +485,10 @@
     def turn(i):
         across_wait(back_z_r, i, bz_rsem)
         back_x[i] = grouped(from_groups(back_z_r, back_z_s, i))
-        fan_out(back_x, i, ret, HALF - CROSS + i, b_ssem, b_rsem, bown_sem)
+        fan_out(back_x, i, ret, HALF - BACK + i, b_ssem, b_rsem, bown_sem)
 
     def arrive(i):
-        p = HALF - CROSS + i
+        p = HALF - BACK + i
         fan_recv(ret, p, b_rsem, bown_sem)
         x = flat(ret, p)
         put(p, dot(own_hi[...], x, NN) + dot(own_lo[...], x, NN))
@@ -506,7 +519,7 @@
                 copy.wait_recv()
             lax.fori_loop(0, wq, finish_gu, 0)
             lax.fori_loop(0, HALF, finish_d, 0)
-        elif t == 2 * wq + 3:
+        if t == HOME + 1:
             pltpu.make_async_copy(
                 meta_v.at[pl.ds(0, zn - 1)], meta_v.at[pl.ds(0, zn - 1)], m_ssem).wait()
             for copy in weights_out() + grads_out():
@@ -520,25 +533,41 @@
             for i in range(CROSS):
                 fan_wait(send, i, x_ssem)
                 across_wait(z_s, i, z_ssem)
+            for i in range(BACK):
                 across_wait(back_z_s, i, bz_ssem)
 
-    for t in range(RING + long + 1):
+    def when(n, s):
+        return n + s + (1 if s > 0 and n < HOME - 1 else 0)
+
+    for t in range(HOME + long + 1):
         for s in range(long - 1, 0, -1):
-            if 0 <= t - s - 1 < RING:
-                rs_step(t - s - 1, s)
-        if t < RING:
+            for n in range(HOME):
+                if when(n, s) == t:
+                    rs_step(n, s)
+        if t < HOME:
             combine(rings[t])
             rs_step(t, 0)
-        if t > long:
-            rs_final(t - long - 1)
+        for n in range(HOME):
+            if when(n, long) == t:
+                rs_final(n)
         fill(t)
-        if 0 < t <= CROSS:
+        if 0 < t <= BACK:
             turn(t - 1)
-        if RING < t <= RING + CROSS:
-            arrive(t - RING - 1)
-
-    for way in (0, 1):
-        ring_sent(rs_ssem, way)
+        if HOME < t <= HOME + BACK:
+            arrive(t - HOME - 1)
+
+    for n in range(HOME):
+        for way in (0, 1):
+            some = ag.at[0, pl.ds(0, hops(n, way))]
+            pltpu.make_async_copy(some, some, rs_ssem.at[way, n]).wait()
+
+
+def write_out(*refs):
+    copies = [pltpu.make_async_copy(refs[i], refs[5 + i], refs[10].at[i]) for i in range(5)]
+    for copy in copies:
+        copy.start()
+    for copy in copies:
+        copy.wait()
 
 
 def local(zn, en, tokens, cotangent, expert_ids, gate_probs, gate_weight, up_weight, down_weight):
@@ -579,15 +608,15 @@
         vm(group, BF16),
         vm(group, BF16),
         vm((PIECES, zn, tn, w), F32),
-        vm((2, RING, long, tn, w), BF16),
-        vm((2, RING, long, tn, w), BF16),
+        vm((2, HOME, long, tn, w), BF16),
+        vm((2, HOME, long, tn, w), BF16),
         vm((wq, w, 2 * ff), BF16),
         vm((HALF, fh, w), BF16),
         vm((wq, w, 2 * ff), BF16),
         vm((HALF, fh, w), BF16),
         dma((PIECES,)), dma((2 + HALF,)), dma, dma, dma((2 + HALF,)), dma((2 + HALF,)),
         dma((2,)), dma((2, RING, long)), dma((RING,)), dma((RING,)), dma((RING,)),
-        dma((PIECES,)), dma((PIECES,)), dma((PIECES,)), dma((2,)), dma((2, RING, long)),
+        dma((PIECES,)), dma((PIECES,)), dma((PIECES,)), dma((2, HOME)), dma((2, HOME, long)),
         dma((2,)), dma((2,)),
         vm((8, tn), jnp.int32),
         vm((8, tn), F32),
@@ -602,11 +631,11 @@
         vm((CROSS,) + group[1:], BF16),
         vm((CROSS, zn, en * RANKS, w), BF16),
         vm((CROSS, zn, en * RANKS, w), BF16),
-        vm((CROSS, zn, en * RANKS, w), BF16),
-        vm((CROSS, zn, en * RANKS, w), BF16),
-        vm((CROSS,) + group[1:], BF16),
+        vm((BACK, zn, en * RANKS, w), BF16),
+        vm((BACK, zn, en * RANKS, w), BF16),
+        vm((BACK,) + group[1:], BF16),
         dma((2,)), dma((CROSS,)), dma((CROSS,)), dma((CROSS,)), dma((CROSS,)), dma((CROSS,)),
-        dma((CROSS,)), dma((CROSS,)),
+        dma((BACK,)), dma((BACK,)),
     ]
     hbm = pl.BlockSpec(memory_space=pl.ANY)
     y, dx, g, u, dd = pl.pallas_call(
@@ -628,6 +657,16 @@
         expert_ids.T, gate_probs.T, tokens, cotangent,
         gate_weight.reshape(wq, w, ff), up_weight.reshape(wq, w, ff), down_weight.reshape(fh, d),
     )
+    made = [pltpu.with_memory_space_constraint(a, pltpu.VMEM) for a in (y, dx, g, u, dd)]
+    y, dx, g, u, dd = pl.pallas_call(
+        write_out,
+        out_shape=tuple(jax.ShapeDtypeStruct(a.shape, BF16) for a in made),
+        in_specs=[pl.BlockSpec(memory_space=pltpu.VMEM)] * 5,
+        out_specs=(hbm,) * 5,
+        scratch_shapes=[dma((5,))],
+        name="write_out",
+        compiler_params=pltpu.CompilerParams(vmem_limit_bytes=1 << 20),
+    )(*made)
     return y, dx, g.reshape(1, wq * w, ff), u.reshape(1, wq * w, ff), dd.reshape(1, fh, d)
 
 

time: 109 us -> 104 us (0.954)
  local copies, waits for them, and re-layouts: 4.74 us -> 0 us
    unnamed x5 -> x0, local copies, waits for them, and re-layouts: 4.74 us -> none
    pallas_call x1, Pallas kernels: 103 us -> 100 us  [local(): pl.pallas_call(functools.partial(kernel, zn, en), out_shape=(pltpu.VMEM((...]
    pallas_call x0 -> x1, Pallas kernels: none -> 2.31 us  [local(): pl.pallas_call(write_out, out_shape=tuple((jax.ShapeDtypeStruct(a.shape,...]
where the time goes in v4:
time: 104 us; the launch traced here: 103 us
  Pallas kernels  103 us (99%)
    pallas_call x1, Pallas kernels, local(): pl.pallas_call(functools.partial(kernel, zn, en), out_shape=(pltpu.VMEM((...  100 us
    pallas_call x1, Pallas kernels, local(): pl.pallas_call(write_out, out_shape=tuple((jax.ShapeDtypeStruct(a.shape,...  2.31 us

profile of v4, /device:TPU:2, one launch (start us, length us, event | category | flops | bytes accessed | tf_op | source)
XLA Modules:
  0.0 103.2 jit_solution(16024578403234721373)
XLA Ops:
  0.6 100.2 %moe.1 = (bf16[32,2048]{1,0:T(8,128)(2,1)S(1)}, bf16[32,2048]{1,0:T(8,128)(2,1)S(1)}, bf16[2,512,768]{2,1,0:T(8,128)(2,1)S(1)}, bf16[2,512,768]{2,1,0:T(8,128)(2,1)S(1)}, bf16[384,2048]{1,0:T(8,128)(2,1)S(1)}) custom-call(s32[8,32]{1,0:T(8,128)} %bitcast.11, f32[8,32]{1,0:T(8,128)} %bitcast.12, bf16[32,2048]{1,0:T(8,128)(2,1)} %tok.1, bf16[32,2048]{1,0:T(8,128)(2,1)} %cot.1, ...), custom_call_target="tpu_custom_call" | custom-call | tf_op jit(solution)/shard_map/moe/pallas_call | solution.py:641
  100.9 2.3 %write_out.1 = (bf16[32,2048]{1,0:T(8,128)(2,1)}, bf16[32,2048]{1,0:T(8,128)(2,1)}, bf16[2,512,768]{2,1,0:T(8,128)(2,1)}, bf16[2,512,768]{2,1,0:T(8,128)(2,1)}, bf16[384,2048]{1,0:T(8,128)(2,1)}) custom-call(bf16[32,2048]{1,0:T(8,128)(2,1)S(1)} %get-tuple-element.15.refs_0_, bf16[32,2048]{1,0:T(8,128)(2,1)S(1)} %get-tuple-element.16.refs_1_, ...), custom_call_target="tpu_custom_call" | custom-call | tf_op jit(solution)/shard_map/write_out/pallas_call | solution.py:661

commit v5 on v4

--- a/solution.py
+++ b/solution.py
@@ -52,6 +52,7 @@
     lanes = 128
     per = lanes // tn
     long = zn // 2
+    near = en * RANKS
 
     def hops(p, way):
         return long if (p % 2) == way else zn - 1 - long
@@ -87,7 +88,7 @@
     ]
     for copy in tables_in:
         copy.start()
-    for p in list(range(RING, PIECES)) + list(range(RING)):
+    for p in [0] + list(range(RING, PIECES)) + list(range(1, RING)):
         local(p).start()
     wq = HALF // 2
     half_gate = pl.ds(r * wq, wq)
@@ -102,50 +103,51 @@
     for copy in w_local:
         copy.start()
 
-    lane = lax.broadcasted_iota(jnp.int32, (tn, lanes), 1)
-    token = lax.broadcasted_iota(jnp.int32, (tn, lanes), 0)
-    spot = ((lane % tn == token) & (lane // tn == lax.rem(z, per))).astype(F32)
-    for copy in tables_in:
-        copy.wait()
-    for i, table in enumerate((ids_v[...].astype(F32), chance_v[...])):
-        meta_v[z, 8 * i:8 * i + 8, :] = lax.dot_general(
-            table, spot, (NN, ((), ())), precision=lax.Precision.HIGHEST, preferred_element_type=F32)
-
-    row = lax.broadcasted_iota(jnp.int32, (lanes, lanes), 0)
-    col = lax.broadcasted_iota(jnp.int32, (lanes, lanes), 1)
-    before = ((row < col) & (row // tn == col // tn)).astype(F32).astype(BF16)
-    expert = lax.broadcasted_iota(jnp.int32, (en * zn, tn), 0).astype(F32)
-    named = jnp.zeros((en * zn, tn), F32)
-    weight = jnp.zeros((en * zn, tn), F32)
-    for k in range(8):
-        hit = ids_v[k:k + 1, :].astype(F32) == expert
-        named = named + jnp.where(hit, 1.0, 0.0)
-        weight = weight + jnp.where(hit, chance_v[k:k + 1, :], 0.0)
-    rank = dot(named.astype(BF16), before[:tn, :tn], NN)
-    all_rank[...] = jnp.where(named > 0.0, rank, -1.0)
-    all_prob[...] = weight
-    for e in range(en):
-        seen = all_rank[pl.ds(e, zn, stride=en), :]
-        worth = all_prob[pl.ds(e, zn, stride=en), :]
-        for k in range(RANKS):
-            at = slice((e * RANKS + k) * zn, (e * RANKS + k + 1) * zn)
-            own_f[at, :] = jnp.where(seen == float(k), 1.0, 0.0)
-            own_prob[at, :] = jnp.where(seen == float(k), worth, 0.0)
-    own_pick[...] = own_f[...].astype(BF16)
-    near = en * RANKS
-    row = lax.broadcasted_iota(jnp.int32, (slots, slots), 0)
-    col = lax.broadcasted_iota(jnp.int32, (slots, slots), 1)
-    order[...] = ((row // near == col % zn) & (row % near == col // zn)).astype(F32).astype(BF16)
     pl.semaphore_wait(barrier, 1 + (zn - 1) + (en - 1))
 
-
-    def send_meta(d, carry):
-        pltpu.make_async_remote_copy(
-            src_ref=meta_v.at[z], dst_ref=meta_v.at[z], send_sem=m_ssem, recv_sem=m_rsem,
-            device_id={"grp": lax.rem(z + d, zn)}, device_id_type=MESH).start()
-        return carry
-
-    lax.fori_loop(1, zn, send_meta, 0)
+    def own_tables():
+        lane = lax.broadcasted_iota(jnp.int32, (tn, lanes), 1)
+        token = lax.broadcasted_iota(jnp.int32, (tn, lanes), 0)
+        spot = ((lane % tn == token) & (lane // tn == lax.rem(z, per))).astype(F32)
+        for copy in tables_in:
+            copy.wait()
+        for i, table in enumerate((ids_v[...].astype(F32), chance_v[...])):
+            meta_v[z, 8 * i:8 * i + 8, :] = lax.dot_general(
+                table, spot, (NN, ((), ())), precision=lax.Precision.HIGHEST, preferred_element_type=F32)
+
+        row = lax.broadcasted_iota(jnp.int32, (lanes, lanes), 0)
+        col = lax.broadcasted_iota(jnp.int32, (lanes, lanes), 1)
+        before = ((row < col) & (row // tn == col // tn)).astype(F32).astype(BF16)
+        expert = lax.broadcasted_iota(jnp.int32, (en * zn, tn), 0).astype(F32)
+        named = jnp.zeros((en * zn, tn), F32)
+        weight = jnp.zeros((en * zn, tn), F32)
+        for k in range(8):
+            hit = ids_v[k:k + 1, :].astype(F32) == expert
+            named = named + jnp.where(hit, 1.0, 0.0)
+            weight = weight + jnp.where(hit, chance_v[k:k + 1, :], 0.0)
+        rank = dot(named.astype(BF16), before[:tn, :tn], NN)
+        all_rank[...] = jnp.where(named > 0.0, rank, -1.0)
+        all_prob[...] = weight
+        for e in range(en):
+            seen = all_rank[pl.ds(e, zn, stride=en), :]
+            worth = all_prob[pl.ds(e, zn, stride=en), :]
+            for k in range(RANKS):
+                at = slice((e * RANKS + k) * zn, (e * RANKS + k + 1) * zn)
+                own_f[at, :] = jnp.where(seen == float(k), 1.0, 0.0)
+                own_prob[at, :] = jnp.where(seen == float(k), worth, 0.0)
+        own_pick[...] = own_f[...].astype(BF16)
+        row = lax.broadcasted_iota(jnp.int32, (slots, slots), 0)
+        col = lax.broadcasted_iota(jnp.int32, (slots, slots), 1)
+        order[...] = ((row // near == col % zn) & (row % near == col // zn)).astype(F32).astype(BF16)
+
+
+        def send_meta(d, carry):
+            pltpu.make_async_remote_copy(
+                src_ref=meta_v.at[z], dst_ref=meta_v.at[z], send_sem=m_ssem, recv_sem=m_rsem,
+                device_id={"grp": lax.rem(z + d, zn)}, device_id_type=MESH).start()
+            return carry
+
+        lax.fori_loop(1, zn, send_meta, 0)
 
     def ring(p, way, s):
         block = lax.rem(z - step(way) * s + zn, zn)
@@ -330,6 +332,7 @@
             if 0 <= t - s < RING:
                 ring_step(t - s, s)
         if t == 0:
+            own_tables()
             for i in range(CROSS):
                 local(RING + i).wait()
                 send[RING + i] = grouped(select_own(i))
@@ -537,7 +540,7 @@
                 across_wait(back_z_s, i, bz_ssem)
 
     def when(n, s):
-        return n + s + (1 if s > 0 and n < HOME - 1 else 0)
+        return n + s + (1 if s > 0 and n < HOME - 2 else 0)
 
     for t in range(HOME + long + 1):
         for s in range(long - 1, 0, -1):

time: 104 us -> 102 us (0.981)
  Pallas kernels: 103 us -> 101 us
    pallas_call x1, Pallas kernels: 100 us -> 98.9 us  [local(): pl.pallas_call(functools.partial(kernel, zn, en), out_shape=(pltpu.VMEM((...]
where the time goes in v5:
time: 102 us
  Pallas kernels  101 us (99%)
    pallas_call x1, Pallas kernels, local(): pl.pallas_call(functools.partial(kernel, zn, en), out_shape=(pltpu.VMEM((...  98.9 us
    pallas_call x1, Pallas kernels, local(): pl.pallas_call(write_out, out_shape=tuple((jax.ShapeDtypeStruct(a.shape,...  2.31 us

profile of v5, /device:TPU:2, one launch (start us, length us, event | category | flops | bytes accessed | tf_op | source)
XLA Modules:
  0.0 101.9 jit_solution(7199717073591054218)
XLA Ops:
  0.6 98.9 %moe.1 = (bf16[32,2048]{1,0:T(8,128)(2,1)S(1)}, bf16[32,2048]{1,0:T(8,128)(2,1)S(1)}, bf16[2,512,768]{2,1,0:T(8,128)(2,1)S(1)}, bf16[2,512,768]{2,1,0:T(8,128)(2,1)S(1)}, bf16[384,2048]{1,0:T(8,128)(2,1)S(1)}) custom-call(s32[8,32]{1,0:T(8,128)} %bitcast.11, f32[8,32]{1,0:T(8,128)} %bitcast.12, bf16[32,2048]{1,0:T(8,128)(2,1)} %tok.1, bf16[32,2048]{1,0:T(8,128)(2,1)} %cot.1, ...), custom_call_target="tpu_custom_call" | custom-call | tf_op jit(solution)/shard_map/moe/pallas_call | solution.py:644
  99.6 2.3 %write_out.1 = (bf16[32,2048]{1,0:T(8,128)(2,1)}, bf16[32,2048]{1,0:T(8,128)(2,1)}, bf16[2,512,768]{2,1,0:T(8,128)(2,1)}, bf16[2,512,768]{2,1,0:T(8,128)(2,1)}, bf16[384,2048]{1,0:T(8,128)(2,1)}) custom-call(bf16[32,2048]{1,0:T(8,128)(2,1)S(1)} %get-tuple-element.15.refs_0_, bf16[32,2048]{1,0:T(8,128)(2,1)S(1)} %get-tuple-element.16.refs_1_, ...), custom_call_target="tpu_custom_call" | custom-call | tf_op jit(solution)/shard_map/write_out/pallas_call | solution.py:664
